TPU v7x, 256 devices: a whole 4x4x8 slice. The times are simulated.
256 devices in a mesh: snap: 8 (over x, core), lag: 32 (over z, y).
Axes of the slice: x: 4, y: 4, z: 8, core: 2. Of those that a mesh axis runs over, the one named last changes fastest.
Arguments:
- snapshots: bfloat16 [2, 32768, 256], P(None, 'snap', 'lag')
- positions: int32 [256], replicated, may hold values from 0 to 16383, as said below
- counts: int32 [8], P('snap'), may hold values from 1 to 4096, 16384 in all
- initial: float32 [2, 96, 16384], P(None, None, 'lag'), may hold values from -6 to 6
Outputs:
- lag_corr: float32 [2, 16384], P(None, 'lag')
- subspace: float32 [2, 96, 16384], P(None, None, 'lag')
Inputs may be any that keep to these rules, and one draw needn't show every extreme that they name: `positions`: positions are distinct; 0 and 16383 are among them.
All inputs are finite; a program needn't handle non-finite values. No bound on the sum of `counts` on one device may be relied on, other than what follows from the above.
Results may differ from a plain program's by a relative error of at most 0.0003.
Values may be sent and summed in bfloat16 or wider, within the bound.
A program may use at most 64 MiB of HBM per device.

v0:
```python
import functools
import math

import jax
import jax.numpy as jnp
import numpy as np
from jax import lax
from jax.experimental import pallas as pl
from jax.experimental.pallas import tpu as pltpu
from jax.sharding import PartitionSpec as P

MESH = pl.DeviceIdType.MESH
F32 = jnp.float32
BF16 = jnp.bfloat16
ITERS = 2
SENSORS = 256
LAGS = 16384
ROWS = 4096
COLUMNS = 96
N_SNAP = 8
N_LAG = 32
OWN = COLUMNS // N_SNAP
LANES = 128
PADDED = 2 * LAGS
FIRST = PADDED // LANES
HALF = LAGS // LANES
PER = HALF // N_LAG

SNAPS, CORR, CORR_ALL, BINS, LAGCORR, COLS = range(6)
IMAGE, IMAGE_ALL, GRAM, GRAM_ALL = range(6, 10)
PHASES = 6 + 4 * ITERS


def tables():
    rows = np.arange(2 * HALF)
    owner, part, place = rows // (2 * PER), rows // PER % 2, rows % PER
    lag_row = owner * PER + place
    first = np.arange(FIRST)
    lane = np.arange(LANES)
    turn = 2.0 * math.pi * (np.outer(first, lag_row) % FIRST) / FIRST
    cosine, sine = np.cos(turn), np.sin(turn)
    real = part[None, :] == 0
    forward = np.concatenate([np.where(real, cosine, sine), np.where(real, -sine, cosine)], 0)
    backward = np.concatenate(
        [np.where(real, cosine, sine).T, np.where(real, -sine, cosine).T], 1
    )
    small = 2.0 * math.pi * (np.outer(lane, lane) % LANES) / LANES
    c, s = np.cos(small), np.sin(small)
    across = np.block([[c, -s], [s, c]])
    back = np.block([[c, s], [-s, c]])
    twist = 2.0 * math.pi * np.outer(first, lane) / PADDED
    twists = np.stack([np.cos(twist), np.sin(twist)])
    return tuple(t.astype(np.float32) for t in (forward, across, back, backward, twists))


def dot(a, b, precision=lax.Precision.HIGHEST):
    return lax.dot_general(a, b, (((1,), (0,)), ((), ())), precision=precision, preferred_element_type=F32)


def dot_nt(a, b, precision=lax.Precision.HIGHEST):
    return lax.dot_general(a, b, (((1,), (1,)), ((), ())), precision=precision, preferred_element_type=F32)


def inverse_factor(gram):
    rows = lax.broadcasted_iota(jnp.int32, (COLUMNS, LANES), 0)
    cols = lax.broadcasted_iota(jnp.int32, (COLUMNS, LANES), 1)
    lane = lax.broadcasted_iota(jnp.int32, (1, LANES), 1)
    state = gram
    for j in range(COLUMNS - 1):
        row = state[j : j + 1, :]
        scale = 1.0 / row[:, j : j + 1]
        multiplier = jnp.where(rows[:, :1] > j, state[:, j : j + 1] * scale, 0.0)
        row = jnp.where(lane == j, 1.0, row)
        state = jnp.where((cols == j) & (rows > j), 0.0, state) - multiplier * row
    diagonal = jnp.sum(jnp.where(rows == cols, state, 0.0), axis=1, keepdims=True)
    unit = jnp.where(cols < rows, state, jnp.where(cols == rows, 1.0, 0.0))
    return unit * (1.0 / jnp.sqrt(diagonal))


def kernel(
    counts, positions, snaps, initial, forward, across, back, backward, twists,
    lag_out, sub_out,
    snap_send, snap_recv, corr_send, corr_recv, row_send, row_recv, bin_send, bin_recv,
    lag_send, lag_recv, col_recv, image_send, image_all, gram_send, gram_recv, tile_send, gram_all,
    send_sems, recv_sems,
):
    me, block = lax.axis_index("lag"), lax.axis_index("snap")
    mine = (3 * me + 7) // 8
    active = (8 * mine) // 3 == me
    own_col = jnp.minimum(mine, OWN - 1)

    def along(axis, size, here, act):
        def body(k, carry):
            act(lax.rem(here + k, size))
            return carry

        lax.fori_loop(1, size, body, 0)

    def send(phase, src, dst, axis, peer):
        pltpu.make_async_remote_copy(
            src_ref=src, dst_ref=dst, send_sem=send_sems.at[phase], recv_sem=recv_sems.at[phase],
            device_id={axis: peer}, device_id_type=MESH,
        ).start()

    def to_lags(phase, src_of, dst):
        along("lag", N_LAG, me, lambda p: send(phase, src_of(p), dst, "lag", p))

    def to_snaps(phase, src, dst):
        along("snap", N_SNAP, block, lambda p: send(phase, src, dst, "snap", p))

    def to_owners(phase, src_of, dst):
        def body(k, carry):
            j = lax.rem(own_col + k, OWN)
            owner = (8 * j) // 3

            @pl.when(owner != me)
            def _():
                send(phase, src_of(j), dst, "lag", owner)

            return carry

        lax.fori_loop(0, OWN, body, 0)

    def wait(sems, phase, ref):
        pltpu.make_async_copy(ref, ref, sems.at[phase]).wait()

    barrier = pltpu.get_barrier_semaphore()
    along("lag", N_LAG, me, lambda p: pl.semaphore_signal(
        barrier, inc=1, device_id={"lag": p}, device_id_type=MESH))
    along("snap", N_SNAP, block, lambda p: pl.semaphore_signal(
        barrier, inc=1, device_id={"snap": p}, device_id_type=MESH))

    live = lax.broadcasted_iota(jnp.int32, (8, ROWS), 1) < counts[0]
    for c in range(2):
        snap_send[c] = jnp.where(live, snaps[c].astype(F32), 0.0).astype(BF16)
    pl.semaphore_wait(barrier, N_LAG + N_SNAP - 2)

    def snap_piece(p):
        return snap_send.at[:, :, pl.ds(pl.multiple_of(p * LANES, LANES), LANES)]

    to_lags(SNAPS, snap_piece, snap_recv.at[me])
    snap_recv[me] = snap_send[:, :, pl.ds(pl.multiple_of(me * LANES, LANES), LANES)]
    to_owners(COLS, lambda j: initial.at[j], col_recv.at[me])

    @pl.when(active)
    def _():
        col_recv[me] = initial[own_col]

    wait(recv_sems, SNAPS, snap_recv.at[pl.ds(0, N_LAG - 1)])
    x = [snap_recv[:, c].astype(F32).reshape(SENSORS, LANES) for c in range(2)]
    left = jnp.concatenate([x[0], x[1]], 1).astype(BF16)
    turned = jnp.concatenate([x[1], -x[0]], 1).astype(BF16)
    real = dot_nt(left, left, None)
    imag = dot_nt(turned, left, None)
    square = (SENSORS, SENSORS)
    below = lax.broadcasted_iota(jnp.int32, square, 0) >= lax.broadcasted_iota(jnp.int32, square, 1)
    corr_send[...] = jnp.where(below, real, imag)

    def rows_of(p):
        return pl.ds(pl.multiple_of(p * 8, 8), 8)

    to_lags(CORR, lambda p: corr_send.at[rows_of(p)], corr_recv.at[me])
    corr_recv[me] = corr_send[rows_of(me), :]

    strip = (8, SENSORS)
    sensor = me * 8 + lax.broadcasted_iota(jnp.int32, strip, 0)
    other = lax.broadcasted_iota(jnp.int32, strip, 1)
    place = jnp.broadcast_to(positions[...], strip).astype(F32)
    own_place = jnp.sum(jnp.where(sensor == other, place, 0.0), axis=1, keepdims=True)
    gap = own_place - place
    lags = jnp.abs(gap).astype(jnp.int32)
    lower = sensor >= other
    high = lags // LANES
    target = (high // PER) * (2 * PER) + jnp.where(lower, 0, PER) + high % PER
    low = lags % LANES
    sign = jnp.where(lower | (gap > 0.0), 1.0, -1.0)

    wait(recv_sems, CORR, corr_recv.at[pl.ds(0, N_LAG - 1)])
    row_send[:, :SENSORS] = jnp.sum(corr_recv[...], axis=0)
    row_send[:, SENSORS:] = jnp.full((8, LANES), counts[0].astype(F32), F32)
    row_recv[block] = row_send[...]
    to_snaps(CORR_ALL, row_send, row_recv.at[block])
    wait(recv_sems, CORR_ALL, row_recv.at[pl.ds(0, N_SNAP - 1)])
    summed = jnp.sum(row_recv[...], axis=0)
    values = summed[:, :SENSORS] * sign
    total = summed[:, SENSORS:]

    row_ids = lax.broadcasted_iota(jnp.int32, (2 * HALF, SENSORS), 0)
    lane_ids = lax.broadcasted_iota(jnp.int32, (LANES, SENSORS), 0)
    part_0 = values.astype(BF16).astype(F32)
    part_1 = (values - part_0).astype(BF16).astype(F32)
    part_2 = values - part_0 - part_1
    high_hot, low_hot = [], []
    for r in range(8):
        one = slice(r, r + 1)
        high_hot.append(jnp.where(row_ids == target[one], 1.0, 0.0).astype(BF16))
        hit = lane_ids == low[one]
        low_hot.append(
            jnp.concatenate(
                [jnp.where(hit, part[one], 0.0).astype(BF16) for part in (part_0, part_1, part_2)]
                + [jnp.where(hit, 1.0, 0.0).astype(BF16)],
                0,
            )
        )
    bins = dot_nt(jnp.concatenate(high_hot, 1), jnp.concatenate(low_hot, 1), None)
    bin_send[:, :LANES] = bins[:, :LANES] + bins[:, LANES : 2 * LANES] + bins[:, 2 * LANES : 3 * LANES]
    bin_send[:, LANES:] = bins[:, 3 * LANES :]
    to_lags(BINS, lambda p: bin_send.at[rows_of(p)], bin_recv.at[me])
    bin_recv[me] = bin_send[rows_of(me), :]
    wait(recv_sems, BINS, bin_recv.at[pl.ds(0, N_LAG - 1)])
    lag_sums = jnp.sum(bin_recv[...], axis=0)
    lag_corr = lag_sums[:, :LANES] / (jnp.maximum(lag_sums[:, LANES:], 1.0) * total)
    lag_send[...] = lag_corr
    to_lags(LAGCORR, lambda p: lag_send, lag_recv.at[me])
    lag_recv[me] = lag_corr
    for c in range(2):
        for r in range(PER):
            lag_out[c : c + 1, r * LANES : (r + 1) * LANES] = lag_corr[c * PER + r : c * PER + r + 1, :]
    wait(recv_sems, LAGCORR, lag_recv.at[pl.ds(0, N_LAG - 1)])

    def rising(v):
        a = dot(forward[...], v)
        ar, ai = a[:FIRST], a[FIRST:]
        tc, ts = twists[0], twists[1]
        return jnp.concatenate([ar * tc + ai * ts, ai * tc - ar * ts], 1)

    def apply(v, spectrum):
        e = dot(dot(rising(v), across[...]) * spectrum, back[...])
        er, ei = e[:, :LANES], e[:, LANES:]
        tc, ts = twists[0], twists[1]
        return dot(backward[...], jnp.concatenate([er * tc - ei * ts, ei * tc + er * ts], 0))

    whole = lag_recv[...].reshape(2 * HALF, LANES)
    ids = [lax.broadcasted_iota(jnp.int32, (2 * HALF, LANES), d) for d in range(2)]
    head = (ids[0] == 0) & (ids[1] == 0)
    whole = jnp.where(head, 0.5 * whole, whole)
    half_spectrum = dot(rising(whole), across[:, :LANES]) * (2.0 / PADDED)
    spectrum = jnp.concatenate([half_spectrum, half_spectrum], 1)

    @pl.when(active)
    def _():
        wait(recv_sems, COLS, col_recv.at[pl.ds(0, N_LAG - 1)])

    column = jnp.where(active, col_recv[...].reshape(2 * HALF, LANES), 0.0)
    for sweep in range(ITERS):
        column = apply(column, spectrum)
        image_send[sweep] = column
        slot = image_all.at[sweep, block * OWN + own_col]

        @pl.when(active)
        def _():
            to_lags(IMAGE + 4 * sweep, lambda p: image_send.at[sweep, rows_of(p)], slot)
            image_all[sweep, block * OWN + own_col] = image_send[sweep, rows_of(me), :]

    def gathered(sweep):
        group = image_all.at[sweep, pl.ds(block * OWN, OWN)]

        @pl.when(active)
        def _():
            wait(recv_sems, IMAGE + 4 * sweep, image_all.at[sweep, pl.ds(0, OWN - 1)])

        @pl.when(jnp.logical_not(active))
        def _():
            wait(recv_sems, IMAGE + 4 * sweep, image_all.at[sweep, pl.ds(0, OWN)])

        to_snaps(IMAGE_ALL + 4 * sweep, group, group)
        wait(recv_sems, IMAGE_ALL + 4 * sweep, image_all.at[sweep, pl.ds(0, COLUMNS - OWN)])
        return jnp.concatenate([image_all[sweep, :, i, :] for i in range(2 * PER)], 1)

    def orthonormal(sweep, mapped):
        partial = dot_nt(mapped, mapped) * (1.0 / LAGS)
        gram_send[sweep, :, :COLUMNS] = partial
        gram_send[sweep, :, COLUMNS:] = jnp.zeros((COLUMNS, LANES - COLUMNS), F32)
        to_owners(GRAM + 4 * sweep, lambda j: gram_send.at[sweep, rows_of(j)], gram_recv.at[sweep, me])

        @pl.when(active)
        def _():
            gram_recv[sweep, me] = gram_send[sweep, rows_of(own_col), :]
            wait(recv_sems, GRAM + 4 * sweep, gram_recv.at[sweep, pl.ds(0, N_LAG - 1)])
            tile_send[sweep] = jnp.sum(gram_recv[sweep], axis=0)
            gram_all[sweep, own_col] = tile_send[sweep]
            to_lags(GRAM_ALL + 4 * sweep, lambda p: tile_send.at[sweep], gram_all.at[sweep, own_col])
            wait(recv_sems, GRAM_ALL + 4 * sweep, gram_all.at[sweep, pl.ds(0, OWN - 1)])

        @pl.when(jnp.logical_not(active))
        def _():
            wait(recv_sems, GRAM_ALL + 4 * sweep, gram_all.at[sweep, pl.ds(0, OWN)])

        inverse = inverse_factor(gram_all[sweep].reshape(COLUMNS, LANES))
        return inverse[:, :COLUMNS]

    inverse = orthonormal(0, gathered(0))
    mapped = dot(inverse, gathered(1))
    result = dot(orthonormal(1, mapped), mapped)
    for c in range(2):
        sub_out[c] = result[:, c * PER * LANES : (c + 1) * PER * LANES]

    wait(send_sems, SNAPS, snap_recv.at[pl.ds(0, N_LAG - 1)])
    wait(send_sems, CORR, corr_recv.at[pl.ds(0, N_LAG - 1)])
    wait(send_sems, CORR_ALL, row_recv.at[pl.ds(0, N_SNAP - 1)])
    wait(send_sems, BINS, bin_recv.at[pl.ds(0, N_LAG - 1)])
    wait(send_sems, LAGCORR, lag_recv.at[pl.ds(0, N_LAG - 1)])

    @pl.when(active)
    def _():
        wait(send_sems, COLS, col_recv.at[pl.ds(0, OWN - 1)])
        for sweep in range(ITERS):
            wait(send_sems, IMAGE + 4 * sweep, image_send.at[sweep, pl.ds(0, 2 * HALF - 8)])
            wait(send_sems, GRAM + 4 * sweep, gram_recv.at[sweep, pl.ds(0, OWN - 1)])
            wait(send_sems, GRAM_ALL + 4 * sweep, gram_recv.at[sweep, pl.ds(0, N_LAG - 1)])

    @pl.when(jnp.logical_not(active))
    def _():
        wait(send_sems, COLS, col_recv.at[pl.ds(0, OWN)])
        for sweep in range(ITERS):
            wait(send_sems, GRAM + 4 * sweep, gram_recv.at[sweep, pl.ds(0, OWN)])

    for sweep in range(ITERS):
        wait(send_sems, IMAGE_ALL + 4 * sweep, image_all.at[sweep, pl.ds(0, COLUMNS - OWN)])


def on_device(snapshots, positions, counts, initial):
    snaps = jnp.transpose(snapshots, (0, 2, 1))
    start = lax.axis_index("snap") * OWN
    own = lax.dynamic_slice_in_dim(initial, start, OWN, 1)
    own = jnp.transpose(own.reshape(2, OWN, PER, LANES), (1, 0, 2, 3)).reshape(OWN, 2 * PER, LANES)
    vmem = pl.BlockSpec(memory_space=pltpu.VMEM)
    tile = (2 * PER, LANES)
    return pl.pallas_call(
        kernel,
        out_shape=(
            jax.ShapeDtypeStruct((2, PER * LANES), F32),
            jax.ShapeDtypeStruct((2, COLUMNS, PER * LANES), F32),
        ),
        in_specs=[pl.BlockSpec(memory_space=pltpu.SMEM)] + [vmem] * 8,
        out_specs=(vmem, vmem),
        scratch_shapes=[
            pltpu.VMEM((2, 8, ROWS), BF16),
            pltpu.VMEM((N_LAG, 2, 8, LANES), BF16),
            pltpu.VMEM((SENSORS, SENSORS), F32),
            pltpu.VMEM((N_LAG, 8, SENSORS), F32),
            pltpu.VMEM((8, SENSORS + LANES), F32),
            pltpu.VMEM((N_SNAP, 8, SENSORS + LANES), F32),
            pltpu.VMEM((2 * HALF, 2 * LANES), F32),
            pltpu.VMEM((N_LAG, 8, 2 * LANES), F32),
            pltpu.VMEM(tile, F32),
            pltpu.VMEM((N_LAG, *tile), F32),
            pltpu.VMEM((N_LAG, *tile), F32),
            pltpu.VMEM((ITERS, 2 * HALF, LANES), F32),
            pltpu.VMEM((ITERS, COLUMNS, *tile), F32),
            pltpu.VMEM((ITERS, COLUMNS, LANES), F32),
            pltpu.VMEM((ITERS, N_LAG, *tile), F32),
            pltpu.VMEM((ITERS, *tile), F32),
            pltpu.VMEM((ITERS, OWN, *tile), F32),
            pltpu.SemaphoreType.DMA((PHASES,)),
            pltpu.SemaphoreType.DMA((PHASES,)),
        ],
        compiler_params=pltpu.CompilerParams(
            collective_id=0, has_side_effects=True, vmem_limit_bytes=48 << 20
        ),
        name="coarray_subspace",
    )(counts, positions.reshape(1, SENSORS), snaps, own, *(jnp.asarray(t) for t in tables()))


def solution(mesh):
    return jax.shard_map(
        on_device,
        mesh=mesh,
        in_specs=(P(None, "snap", "lag"), P(None), P("snap"), P(None, None, "lag")),
        out_specs=(P(None, "lag"), P(None, None, "lag")),
        check_vma=False,
    )
```

profile of v0, /device:TPU:1, one launch (start us, length us, event | category | flops | bytes accessed | tf_op | source)
XLA Modules:
  0.0 120.9 jit_solution(8501166321931459044)
XLA Ops:
  0.6 0.0 copy-start
  0.6 0.0 copy-start.3
  1.4 0.3 copy-done
  1.7 0.0 copy-start.7
  1.7 0.0 copy-done.3
  1.7 0.7 copy-done.7
  2.4 0.0 copy-start.1
  2.4 1.0 copy-done.1
  3.4 0.0 copy-start.2
  3.4 1.0 copy-done.2
  4.5 0.0 copy-start.4
  4.5 0.9 copy-done.4
  5.4 0.0 copy-start.5
  5.4 0.9 copy-done.5
  6.4 0.0 copy-start.6
  6.4 0.9 copy-done.6
  7.3 112.3 %coarray_subspace.1 = (f32[2,512]{1,0:T(2,128)S(1)}, f32[2,96,512]{2,1,0:T(8,128)S(1)}) custom-call(s32[1]{0:T(128)S(6)} %copy.15.counts, s32[1,256]{1,0:T(1,128)S(1)} %bitcast.7, bf16[2,8,4096]{2,1,0:T(8,128)(2,1)S(1)} %bitcast.6, f32[12,8,128]{2,1,0:T(8,128)S(1)} %bitcast.5, f32[512,256]{1,0:T(8,128)S(1)} %copy-done.2, f32[256,256]{1,0:T(8,128)S(1)} %copy-done.5, ...), custom_call_target="tpu_custom_call" | custom-call | tf_op jit(solution)/shard_map/coarray_subspace/pallas_call | solution.py:329
  119.6 0.6 copy.16
  120.2 0.7 copy.17
  (3 shorter events, 0.0 us)
Async XLA Ops:
  0.6 1.0 copy-start
  0.6 1.1 copy-start.3
  1.7 0.7 copy-start.7
  2.4 1.0 copy-start.1
  3.4 1.0 copy-start.2
  4.5 0.9 copy-start.4
  5.4 0.9 copy-start.5
  6.4 0.9 copy-start.6
where the time goes:
time: 121 us
  Pallas kernels  112 us (93%)
  local copies, waits for them, and re-layouts  7.22 us (6%)
  between operations  1.41 us (1%)
    pallas_call x1, Pallas kernels, on_device(): pl.pallas_call(kernel, out_shape=(jax.ShapeDtypeStruct((2, PER * LANES),...  112 us
    unnamed x18, local copies, waits for them, and re-layouts  7.18 us

commit v1 on v0

v1 whole, which is shorter than its diff:
```python
import functools
import math

import jax
import jax.numpy as jnp
import numpy as np
from jax import lax
from jax.experimental import pallas as pl
from jax.experimental.pallas import tpu as pltpu
from jax.sharding import PartitionSpec as P

MESH = pl.DeviceIdType.MESH
F32 = jnp.float32
BF16 = jnp.bfloat16
ITERS = 2
SENSORS = 256
LAGS = 16384
ROWS = 4096
COLUMNS = 96
N_SNAP = 8
LAG_Z, LAG_Y = 8, 4
N_LAG = LAG_Z * LAG_Y
OWN = COLUMNS // N_SNAP
LANES = 128
PADDED = 2 * LAGS
FIRST = PADDED // LANES
HALF = LAGS // LANES
PER = HALF // N_LAG

SNAPS, CORR, CORR_ALL, BINS, LAGCORR, COLS, COUNTS, LIVE = range(8)
IMAGE, IMAGE_ALL, GRAM, GRAM_ALL = range(8, 12)
PHASES = 8 + 4 * ITERS
BLOCK = 4


def tables():
    rows = np.arange(2 * HALF)
    owner, part, place = rows // (2 * PER), rows // PER % 2, rows % PER
    lag_row = owner * PER + place
    first = np.arange(FIRST)
    lane = np.arange(LANES)
    turn = 2.0 * math.pi * (np.outer(first, lag_row) % FIRST) / FIRST
    cosine, sine = np.cos(turn), np.sin(turn)
    real = part[None, :] == 0
    forward = np.concatenate([np.where(real, cosine, sine), np.where(real, -sine, cosine)], 0)
    backward = np.concatenate(
        [np.where(real, cosine, sine).T, np.where(real, -sine, cosine).T], 1
    )
    small = 2.0 * math.pi * (np.outer(lane, lane) % LANES) / LANES
    c, s = np.cos(small), np.sin(small)
    across = np.block([[c, -s], [s, c]])
    back = np.block([[c, s], [-s, c]])
    twist = 2.0 * math.pi * np.outer(first, lane) / PADDED
    twists = np.stack([np.cos(twist), np.sin(twist)])
    return tuple(t.astype(np.float32) for t in (forward, across, back, backward, twists))


def dot(a, b, precision=lax.Precision.HIGHEST):
    return lax.dot_general(a, b, (((1,), (0,)), ((), ())), precision=precision, preferred_element_type=F32)


def dot_nt(a, b, precision=lax.Precision.HIGHEST):
    return lax.dot_general(a, b, (((1,), (1,)), ((), ())), precision=precision, preferred_element_type=F32)


def inverse_factor(gram):
    shape = (8, LANES)
    sub = lax.broadcasted_iota(jnp.int32, shape, 0)
    lane = lax.broadcasted_iota(jnp.int32, shape, 1)
    tiles = [gram[8 * t : 8 * t + 8, :] for t in range(COLUMNS // 8)]
    pivots = [jnp.ones(shape, F32) for _ in tiles]

    def spread(x):
        return jnp.broadcast_to(x, shape)

    for start in range(0, COLUMNS, BLOCK):
        t, first = divmod(start, 8)
        own = tiles[t]
        inside = (lane >= start) & (lane < start + BLOCK)
        s = [
            [spread(own[first + k : first + k + 1, start + m : start + m + 1]) for m in range(k + 1)]
            for k in range(BLOCK)
        ]
        rows = []
        for k in range(BLOCK):
            row = jnp.where(inside, 0.0, spread(own[first + k : first + k + 1, :]))
            rows.append(jnp.where(lane == start + k, 1.0, row))
        inverses = []
        for m in range(BLOCK):
            inverses.append(1.0 / s[m][m])
            factors = {k: s[k][m] * inverses[m] for k in range(m + 1, BLOCK)}
            for k in range(m + 1, BLOCK):
                for n in range(m + 1, k + 1):
                    s[k][n] = s[k][n] - factors[k] * s[n][m]
                rows[k] = rows[k] - factors[k] * rows[m]
        for u in range(t, len(tiles)):
            if u == t and first + BLOCK == 8:
                continue
            rest = jnp.where(inside, 0.0, tiles[u])
            cols = [spread(tiles[u][:, start + m : start + m + 1]) for m in range(BLOCK)]
            for m in range(BLOCK):
                multiplier = cols[m] * inverses[m]
                for n in range(m + 1, BLOCK):
                    cols[n] = cols[n] - multiplier * s[n][m]
                rest = rest - multiplier * rows[m]
            tiles[u] = rest
        if first + BLOCK == 8:
            kept = own
        else:
            kept = jnp.where(sub < first, own, tiles[t])
        for k in range(BLOCK):
            kept = jnp.where(sub == first + k, rows[k], kept)
            pivots[t] = jnp.where(sub == first + k, s[k][k], pivots[t])
        tiles[t] = kept
    return jnp.concatenate(
        [
            jnp.where(lane <= 8 * t + sub, tile, 0.0) * (1.0 / jnp.sqrt(pivots[t]))
            for t, tile in enumerate(tiles)
        ],
        0,
    )


def far_first(size):
    return sorted(range(1, size), key=lambda d: -min(d, size - d))


def kernel(
    counts, positions_in, snaps_in, initial_in, forward_in, across_in, back_in, backward_in, twists_in,
    lag_out, sub_out,
    positions, snaps, initial, forward, across, back, backward, twists,
    snap_send, snap_recv, corr_send, corr_recv, row_send, row_recv, bin_send, bin_recv,
    count_send, count_recv, live_send, live_recv, high_hot,
    lag_send, lag_recv, col_send, col_recv, image_send, image_all, gram_send, gram_recv,
    strip_send, gram_all, gram_full,
    send_sems, recv_sems, load_sems,
):
    me, block = lax.axis_index("lag"), lax.axis_index("snap")
    deep, wide = me // LAG_Y, lax.rem(me, LAG_Y)
    mine = (3 * me + 7) // 8
    active = (8 * mine) // 3 == me
    idle = jnp.logical_not(active)
    own_col = jnp.minimum(mine, OWN - 1)
    shifts = [(z, y) for z in range(LAG_Z) for y in range(LAG_Y) if z or y]
    shifts.sort(key=lambda d: -(min(d[0], LAG_Z - d[0]) + min(d[1], LAG_Y - d[1])))

    loads = [
        pltpu.make_async_copy(src, dst, load_sems.at[i])
        for i, (src, dst) in enumerate(
            [
                (snaps_in, snaps), (initial_in, initial), (positions_in, positions), (forward_in, forward),
                (across_in, across), (back_in, back), (backward_in, backward), (twists_in, twists),
            ]
        )
    ]
    for load in loads:
        load.start()

    def all_lags(act):
        for z, y in shifts:
            act(lax.rem(deep + z, LAG_Z) * LAG_Y + lax.rem(wide + y, LAG_Y))

    def all_snaps(act):
        for d in far_first(N_SNAP):
            act(lax.rem(block + d, N_SNAP))

    def send(phase, src, dst, axis, peer):
        pltpu.make_async_remote_copy(
            src_ref=src, dst_ref=dst, send_sem=send_sems.at[phase], recv_sem=recv_sems.at[phase],
            device_id={axis: peer}, device_id_type=MESH,
        ).start()

    def wait(sems, phase, ref):
        pltpu.make_async_copy(ref, ref, sems.at[phase]).wait()

    drains = []

    def drain(phase, ref, senders=None):
        def finish():
            if senders is None:
                wait(send_sems, phase, ref)
            else:
                pl.when(senders)(lambda: wait(send_sems, phase, ref))

        drains.append(finish)

    def to_lags(phase, src_of, dst):
        all_lags(lambda p: send(phase, src_of(p), dst, "lag", p))

    def to_snaps(phase, src, dst):
        all_snaps(lambda p: send(phase, src, dst, "snap", p))

    def rows_of(p):
        return pl.ds(pl.multiple_of(p * 8, 8), 8)

    barrier = pltpu.get_barrier_semaphore()
    all_lags(lambda p: pl.semaphore_signal(barrier, inc=1, device_id={"lag": p}, device_id_type=MESH))
    all_snaps(lambda p: pl.semaphore_signal(barrier, inc=1, device_id={"snap": p}, device_id_type=MESH))

    loads[0].wait()
    live = lax.broadcasted_iota(jnp.int32, (8, ROWS), 1) < counts[0]
    for c in range(2):
        snap_send[c] = jnp.where(live, snaps[c].astype(F32), 0.0).astype(BF16)
    loads[1].wait()
    pair_start = pl.multiple_of((block // 2) * (2 * OWN), 2 * OWN)
    odd = lax.rem(block, 2) == 1
    for c in range(2):
        for r in range(PER):
            pair = initial[c, pl.ds(pair_start, 2 * OWN), r * LANES : (r + 1) * LANES]
            col_send[:, c * PER + r, :] = jnp.where(odd, pair[OWN:], pair[:OWN])
    live_send[...] = jnp.full((8, LANES), counts[0].astype(F32), F32)
    live_recv[block] = live_send[...]
    pl.semaphore_wait(barrier, N_LAG + N_SNAP - 2)

    def snap_piece(p):
        return snap_send.at[:, :, pl.ds(pl.multiple_of(p * LANES, LANES), LANES)]

    to_lags(SNAPS, snap_piece, snap_recv.at[me])
    drain(SNAPS, snap_recv.at[pl.ds(0, N_LAG - 1)])
    snap_recv[me] = snap_send[:, :, pl.ds(pl.multiple_of(me * LANES, LANES), LANES)]
    to_snaps(LIVE, live_send, live_recv.at[block])
    drain(LIVE, live_recv.at[pl.ds(0, N_SNAP - 1)])

    loads[2].wait()
    strip = (8, SENSORS)
    sensor = me * 8 + lax.broadcasted_iota(jnp.int32, strip, 0)
    other = lax.broadcasted_iota(jnp.int32, strip, 1)
    place = jnp.broadcast_to(positions[...], strip).astype(F32)
    own_place = jnp.sum(jnp.where(sensor == other, place, 0.0), axis=1, keepdims=True)
    gap = own_place - place
    lags = jnp.abs(gap).astype(jnp.int32)
    lower = sensor >= other
    high = lags // LANES
    target = (high // PER) * (2 * PER) + jnp.where(lower, 0, PER) + high % PER
    low = lags % LANES
    sign = jnp.where(lower | (gap > 0.0), 1.0, -1.0)
    row_ids = lax.broadcasted_iota(jnp.int32, (2 * HALF, SENSORS), 0)
    lane_ids = lax.broadcasted_iota(jnp.int32, (LANES, SENSORS), 0)
    for r in range(8):
        high_hot[:, r * SENSORS : (r + 1) * SENSORS] = jnp.where(
            row_ids == target[r : r + 1], 1.0, 0.0
        ).astype(BF16)
    hits = jnp.concatenate(
        [jnp.where(lane_ids == low[r : r + 1], 1.0, 0.0).astype(BF16) for r in range(8)], 1
    )
    count_send[...] = dot_nt(high_hot[...], hits, None)
    count_recv[me] = count_send[rows_of(me), :]

    wait(recv_sems, SNAPS, snap_recv.at[pl.ds(0, N_LAG - 1)])
    x = [snap_recv[:, c].astype(F32).reshape(SENSORS, LANES) for c in range(2)]
    left = jnp.concatenate([x[0], x[1]], 1).astype(BF16)
    turned = jnp.concatenate([x[1], -x[0]], 1).astype(BF16)
    real = dot_nt(left, left, None)
    imag = dot_nt(turned, left, None)
    square = (SENSORS, SENSORS)
    below = lax.broadcasted_iota(jnp.int32, square, 0) >= lax.broadcasted_iota(jnp.int32, square, 1)
    corr_send[...] = jnp.where(below, real, imag)
    to_lags(CORR, lambda p: corr_send.at[rows_of(p)], corr_recv.at[me])
    drain(CORR, corr_recv.at[pl.ds(0, N_LAG - 1)])
    corr_recv[me] = corr_send[rows_of(me), :]
    to_lags(COUNTS, lambda p: count_send.at[rows_of(p)], count_recv.at[me])
    drain(COUNTS, count_recv.at[pl.ds(0, N_LAG - 1)])
    for k in range(OWN):
        j = lax.rem(own_col + k, OWN)
        owner = (8 * j) // 3
        pl.when(owner != me)(functools.partial(send, COLS, col_send.at[j], col_recv.at[me], "lag", owner))
    drain(COLS, col_recv.at[pl.ds(0, OWN - 1)], active)
    drain(COLS, col_recv.at[pl.ds(0, OWN)], idle)

    @pl.when(active)
    def _():
        col_recv[me] = col_send[own_col]

    wait(recv_sems, LIVE, live_recv.at[pl.ds(0, N_SNAP - 1)])
    total = jnp.sum(live_recv[...], axis=0)

    wait(recv_sems, CORR, corr_recv.at[pl.ds(0, N_LAG - 1)])
    row_send[...] = jnp.sum(corr_recv[...], axis=0)
    to_snaps(CORR_ALL, row_send, row_recv.at[block])
    drain(CORR_ALL, row_recv.at[pl.ds(0, N_SNAP - 1)])
    row_recv[block] = row_send[...]
    wait(recv_sems, CORR_ALL, row_recv.at[pl.ds(0, N_SNAP - 1)])
    values = jnp.sum(row_recv[...], axis=0) * sign
    part_0 = values.astype(BF16).astype(F32)
    part_1 = (values - part_0).astype(BF16).astype(F32)
    part_2 = values - part_0 - part_1
    low_hot = []
    for r in range(8):
        hit = lane_ids == low[r : r + 1]
        low_hot.append(
            jnp.concatenate(
                [jnp.where(hit, part[r : r + 1], 0.0).astype(BF16) for part in (part_0, part_1, part_2)], 0
            )
        )
    bins = dot_nt(high_hot[...], jnp.concatenate(low_hot, 1), None)
    bin_send[...] = bins[:, :LANES] + bins[:, LANES : 2 * LANES] + bins[:, 2 * LANES :]
    to_lags(BINS, lambda p: bin_send.at[rows_of(p)], bin_recv.at[me])
    drain(BINS, bin_recv.at[pl.ds(0, N_LAG - 1)])
    bin_recv[me] = bin_send[rows_of(me), :]
    wait(recv_sems, COUNTS, count_recv.at[pl.ds(0, N_LAG - 1)])
    divisor = jnp.maximum(jnp.sum(count_recv[...], axis=0), 1.0) * total
    wait(recv_sems, BINS, bin_recv.at[pl.ds(0, N_LAG - 1)])
    lag_corr = jnp.sum(bin_recv[...], axis=0) / divisor
    lag_send[...] = lag_corr
    to_lags(LAGCORR, lambda p: lag_send, lag_recv.at[me])
    drain(LAGCORR, lag_recv.at[pl.ds(0, N_LAG - 1)])
    lag_recv[me] = lag_corr
    for c in range(2):
        for r in range(PER):
            lag_out[c : c + 1, r * LANES : (r + 1) * LANES] = lag_corr[c * PER + r : c * PER + r + 1, :]

    for load in loads[3:]:
        load.wait()

    def rising(v):
        a = dot(forward[...], v)
        ar, ai = a[:FIRST], a[FIRST:]
        tc, ts = twists[0], twists[1]
        return jnp.concatenate([ar * tc + ai * ts, ai * tc - ar * ts], 1)

    def apply(v, spectrum):
        e = dot(dot(rising(v), across[...]) * spectrum, back[...])
        er, ei = e[:, :LANES], e[:, LANES:]
        tc, ts = twists[0], twists[1]
        return dot(backward[...], jnp.concatenate([er * tc - ei * ts, ei * tc + er * ts], 0))

    pl.when(active)(lambda: wait(recv_sems, COLS, col_recv.at[pl.ds(0, N_LAG - 1)]))
    column = jnp.where(active, col_recv[...].reshape(2 * HALF, LANES), 0.0)

    wait(recv_sems, LAGCORR, lag_recv.at[pl.ds(0, N_LAG - 1)])
    whole = lag_recv[...].reshape(2 * HALF, LANES)
    ids = [lax.broadcasted_iota(jnp.int32, (2 * HALF, LANES), d) for d in range(2)]
    whole = jnp.where((ids[0] == 0) & (ids[1] == 0), 0.5 * whole, whole)
    half_spectrum = dot(rising(whole), across[:, :LANES]) * (2.0 / PADDED)
    spectrum = jnp.concatenate([half_spectrum, half_spectrum], 1)

    for sweep in range(ITERS):
        if sweep:
            spectrum = spectrum * (1.0 / (jnp.max(jnp.abs(half_spectrum), keepdims=True) * PADDED))
        column = apply(column, spectrum)
        image_send[sweep] = column
        slot = image_all.at[sweep, block * OWN + own_col]

        @pl.when(active)
        def _():
            to_lags(IMAGE + 4 * sweep, lambda p: image_send.at[sweep, rows_of(p)], slot)
            image_all[sweep, block * OWN + own_col] = image_send[sweep, rows_of(me), :]

        drain(IMAGE + 4 * sweep, image_send.at[sweep, pl.ds(0, 2 * HALF - 8)], active)

    for sweep in range(ITERS):
        group = image_all.at[sweep, pl.ds(block * OWN, OWN)]
        some, every = (image_all.at[sweep, pl.ds(0, n)] for n in (OWN - 1, OWN))
        pl.when(active)(functools.partial(wait, recv_sems, IMAGE + 4 * sweep, some))
        pl.when(idle)(functools.partial(wait, recv_sems, IMAGE + 4 * sweep, every))
        to_snaps(IMAGE_ALL + 4 * sweep, group, group)
        drain(IMAGE_ALL + 4 * sweep, image_all.at[sweep, pl.ds(0, COLUMNS - OWN)])

    images = []
    for sweep in range(ITERS):
        wait(recv_sems, IMAGE_ALL + 4 * sweep, image_all.at[sweep, pl.ds(0, COLUMNS - OWN)])
        image = jnp.concatenate([image_all[sweep, :, i, :] for i in range(2 * PER)], 1)
        own = jnp.concatenate(
            [image_all[sweep, pl.ds(block * OWN, OWN), i, :] for i in range(2 * PER)], 1
        )
        images.append(image)
        gram_send[sweep, :, :COLUMNS] = dot_nt(own, image) * (1.0 / LAGS)
        gram_send[sweep, :, COLUMNS:] = jnp.zeros((OWN, LANES - COLUMNS), F32)
        to_lags(GRAM + 4 * sweep, lambda p: gram_send.at[sweep], gram_recv.at[sweep, me])
        drain(GRAM + 4 * sweep, gram_recv.at[sweep, pl.ds(0, N_LAG - 1)])
        gram_recv[sweep, me] = gram_send[sweep]

    for sweep in range(ITERS):
        wait(recv_sems, GRAM + 4 * sweep, gram_recv.at[sweep, pl.ds(0, N_LAG - 1)])
        strip_send[sweep] = jnp.sum(gram_recv[sweep], axis=0)
        to_snaps(GRAM_ALL + 4 * sweep, strip_send.at[sweep], gram_all.at[sweep, block])
        drain(GRAM_ALL + 4 * sweep, gram_all.at[sweep, pl.ds(0, N_SNAP - 1)])
        gram_all[sweep, block] = strip_send[sweep]

    def whole_gram(sweep):
        wait(recv_sems, GRAM_ALL + 4 * sweep, gram_all.at[sweep, pl.ds(0, N_SNAP - 1)])
        for s in range(N_SNAP):
            gram_full[sweep, s * OWN : (s + 1) * OWN, :] = gram_all[sweep, s]
        return gram_full[sweep]

    inverse = inverse_factor(whole_gram(0))[:, :COLUMNS]
    mapped = dot(inverse, images[1])
    gram = dot_nt(dot(inverse, whole_gram(1)[:, :COLUMNS]), inverse)
    gram = jnp.concatenate([gram, jnp.zeros((COLUMNS, LANES - COLUMNS), F32)], 1)
    result = dot(inverse_factor(gram)[:, :COLUMNS], mapped)
    for c in range(2):
        sub_out[c] = result[:, c * PER * LANES : (c + 1) * PER * LANES]

    for finish in drains:
        finish()


def on_device(snapshots, positions, counts, initial):
    constants = [jnp.asarray(t) for t in tables()]
    operands = (positions.reshape(1, SENSORS), jnp.transpose(snapshots, (0, 2, 1)), initial, *constants)
    vmem = pl.BlockSpec(memory_space=pltpu.VMEM)
    tile = (2 * PER, LANES)
    return pl.pallas_call(
        kernel,
        out_shape=(
            jax.ShapeDtypeStruct((2, PER * LANES), F32),
            jax.ShapeDtypeStruct((2, COLUMNS, PER * LANES), F32),
        ),
        in_specs=[pl.BlockSpec(memory_space=pltpu.SMEM)]
        + [pl.BlockSpec(memory_space=pltpu.HBM)] * len(operands),
        out_specs=(vmem, vmem),
        scratch_shapes=[pltpu.VMEM(a.shape, a.dtype) for a in operands]
        + [
            pltpu.VMEM((2, 8, ROWS), BF16),
            pltpu.VMEM((N_LAG, 2, 8, LANES), BF16),
            pltpu.VMEM((SENSORS, SENSORS), F32),
            pltpu.VMEM((N_LAG, 8, SENSORS), F32),
            pltpu.VMEM((8, SENSORS), F32),
            pltpu.VMEM((N_SNAP, 8, SENSORS), F32),
            pltpu.VMEM((2 * HALF, LANES), F32),
            pltpu.VMEM((N_LAG, *tile), F32),
            pltpu.VMEM((2 * HALF, LANES), F32),
            pltpu.VMEM((N_LAG, *tile), F32),
            pltpu.VMEM((8, LANES), F32),
            pltpu.VMEM((N_SNAP, 8, LANES), F32),
            pltpu.VMEM((2 * HALF, 8 * SENSORS), BF16),
            pltpu.VMEM(tile, F32),
            pltpu.VMEM((N_LAG, *tile), F32),
            pltpu.VMEM((OWN, *tile), F32),
            pltpu.VMEM((N_LAG, *tile), F32),
            pltpu.VMEM((ITERS, 2 * HALF, LANES), F32),
            pltpu.VMEM((ITERS, COLUMNS, *tile), F32),
            pltpu.VMEM((ITERS, OWN, LANES), F32),
            pltpu.VMEM((ITERS, N_LAG, OWN, LANES), F32),
            pltpu.VMEM((ITERS, OWN, LANES), F32),
            pltpu.VMEM((ITERS, N_SNAP, OWN, LANES), F32),
            pltpu.VMEM((ITERS, COLUMNS, LANES), F32),
            pltpu.SemaphoreType.DMA((PHASES,)),
            pltpu.SemaphoreType.DMA((PHASES,)),
            pltpu.SemaphoreType.DMA((len(operands),)),
        ],
        compiler_params=pltpu.CompilerParams(
            collective_id=0, has_side_effects=True, vmem_limit_bytes=48 << 20
        ),
        name="coarray_subspace",
    )(counts, *operands)


def solution(mesh):
    return jax.shard_map(
        on_device,
        mesh=mesh,
        in_specs=(P(None, "snap", "lag"), P(None), P("snap"), P(None, None, "lag")),
        out_specs=(P(None, "lag"), P(None, None, "lag")),
        check_vma=False,
    )
```

time: 121 us -> 93.7 us (0.77)
  Pallas kernels: 112 us -> 83.2 us
  local copies, waits for them, and re-layouts: 7.22 us -> 8.84 us
    pallas_call x1, Pallas kernels: 112 us -> 83.2 us  [on_device(): pl.pallas_call(kernel, out_shape=(jax.ShapeDtypeStruct((2, PER * LANES),...]
    unnamed x18, local copies, waits for them, and re-layouts: 7.18 us -> 8.84 us
where the time goes in v1:
time: 93.7 us; the launch traced here: 93.4 us
  Pallas kernels  83.2 us (89%)
  local copies, waits for them, and re-layouts  8.84 us (9%)
  between operations  1.3 us (1%)
    pallas_call x1, Pallas kernels, on_device(): pl.pallas_call(kernel, out_shape=(jax.ShapeDtypeStruct((2, PER * LANES),...  83.2 us
    unnamed x18, local copies, waits for them, and re-layouts  8.84 us

profile of v1, /device:TPU:1, one launch (start us, length us, event | category | flops | bytes accessed | tf_op | source)
XLA Modules:
  0.0 93.4 jit_solution(2176524360702867208)
XLA Ops:
  1.3 0.0 copy-start.7
  1.3 0.7 copy-done.7
  2.0 0.0 copy-start
  2.0 1.0 %copy-done = f32[256,512]{1,0:T(8,128)S(1)} copy-done((f32[256,512]{1,0:T(8,128)S(1)}, f32[256,512]{1,0:T(8,128)}, u32[]{:S(2)}) %copy-start) | copy-done | bytes 524312
  3.0 0.0 copy-start.1
  3.0 1.0 %copy-done.1 = f32[512,256]{1,0:T(8,128)S(1)} copy-done((f32[512,256]{1,0:T(8,128)S(1)}, f32[512,256]{1,0:T(8,128)}, u32[]{:S(2)}) %copy-start.1) | copy-done | bytes 524312
  4.0 0.0 copy-start.2
  4.0 1.0 %copy-done.2 = f32[2,96,512]{2,1,0:T(8,128)S(1)} copy-done((f32[2,96,512]{2,1,0:T(8,128)S(1)}, f32[2,96,512]{2,1,0:T(8,128)}, u32[]{:S(2)}) %copy-start.2) | copy-done | bytes 393240
  5.0 0.0 copy-start.3
  5.0 0.9 %copy-done.3 = f32[2,256,128]{2,1,0:T(8,128)S(1)} copy-done((f32[2,256,128]{2,1,0:T(8,128)S(1)}, f32[2,256,128]{2,1,0:T(8,128)}, u32[]{:S(2)}) %copy-start.3) | copy-done | bytes 262168
  6.0 0.0 copy-start.4
  6.0 0.9 %copy-done.4 = f32[256,256]{1,0:T(8,128)S(1)} copy-done((f32[256,256]{1,0:T(8,128)S(1)}, f32[256,256]{1,0:T(8,128)}, u32[]{:S(2)}) %copy-start.4) | copy-done | bytes 262168
  6.9 0.0 copy-start.5
  6.9 0.9 %copy-done.5 = f32[256,256]{1,0:T(8,128)S(1)} copy-done((f32[256,256]{1,0:T(8,128)S(1)}, f32[256,256]{1,0:T(8,128)}, u32[]{:S(2)}) %copy-start.5) | copy-done | bytes 262168
  7.9 0.0 copy-start.6
  7.9 0.9 copy-done.6
  8.8 83.2 %coarray_subspace.1 = (f32[2,512]{1,0:T(2,128)S(1)}, f32[2,96,512]{2,1,0:T(8,128)S(1)}) custom-call(s32[1]{0:T(128)S(6)} %copy.13.counts, s32[1,256]{1,0:T(1,128)S(1)} %bitcast.3, bf16[2,8,4096]{2,1,0:T(8,128)(2,1)S(1)} %bitcast.2, f32[2,96,512]{2,1,0:T(8,128)S(1)} %copy-done.2, f32[512,256]{1,0:T(8,128)S(1)} %copy-done.1, f32[256,256]{1,0:T(8,128)S(1)} %copy-done.5, ...), custom_call_target="tpu_custom_call" | custom-call | tf_op jit(solution)/shard_map/coarray_subspace/pallas_call | solution.py:403
  92.0 0.6 copy.14
  92.6 0.7 copy.15
Async XLA Ops:
  1.3 0.7 copy-start.7
  2.0 1.0 %copy-start = (f32[256,512]{1,0:T(8,128)S(1)}, f32[256,512]{1,0:T(8,128)}, u32[]{:S(2)}) copy-start(f32[256,512]{1,0:T(8,128)} %constant.13.clone.backward_in) | copy-start | bytes 1572868
  3.0 1.0 %copy-start.1 = (f32[512,256]{1,0:T(8,128)S(1)}, f32[512,256]{1,0:T(8,128)}, u32[]{:S(2)}) copy-start(f32[512,256]{1,0:T(8,128)} %constant.10.clone.forward_in) | copy-start | bytes 1572868
  4.0 1.0 %copy-start.2 = (f32[2,96,512]{2,1,0:T(8,128)S(1)}, f32[2,96,512]{2,1,0:T(8,128)}, u32[]{:S(2)}) copy-start(f32[2,96,512]{2,1,0:T(8,128)} %initial_in.1) | copy-start | bytes 1179652
  5.0 0.9 %copy-start.3 = (f32[2,256,128]{2,1,0:T(8,128)S(1)}, f32[2,256,128]{2,1,0:T(8,128)}, u32[]{:S(2)}) copy-start(f32[2,256,128]{2,1,0:T(8,128)} %constant.14.clone.twists_in) | copy-start | bytes 786436
  6.0 0.9 %copy-start.4 = (f32[256,256]{1,0:T(8,128)S(1)}, f32[256,256]{1,0:T(8,128)}, u32[]{:S(2)}) copy-start(f32[256,256]{1,0:T(8,128)} %constant.12.clone.back_in) | copy-start | bytes 786436
  6.9 0.9 %copy-start.5 = (f32[256,256]{1,0:T(8,128)S(1)}, f32[256,256]{1,0:T(8,128)}, u32[]{:S(2)}) copy-start(f32[256,256]{1,0:T(8,128)} %constant.11.clone.across_in) | copy-start | bytes 786436
  7.9 0.9 copy-start.6

commit v2 on v1

--- a/solution.py
+++ b/solution.py
@@ -3,6 +3,7 @@
 
 import jax
 import jax.numpy as jnp
+import ml_dtypes
 import numpy as np
 from jax import lax
 from jax.experimental import pallas as pl
@@ -31,6 +32,7 @@
 IMAGE, IMAGE_ALL, GRAM, GRAM_ALL = range(8, 12)
 PHASES = 8 + 4 * ITERS
 BLOCK = 4
+PARTS = 3
 
 
 def tables():
@@ -52,7 +54,14 @@
     back = np.block([[c, s], [-s, c]])
     twist = 2.0 * math.pi * np.outer(first, lane) / PADDED
     twists = np.stack([np.cos(twist), np.sin(twist)])
-    return tuple(t.astype(np.float32) for t in (forward, across, back, backward, twists))
+    split = []
+    for table in (forward, across, back, backward):
+        parts = []
+        for _ in range(PARTS):
+            parts.append(table.astype(ml_dtypes.bfloat16))
+            table = table - parts[-1].astype(np.float64)
+        split.append(np.stack(parts))
+    return (*split, twists.astype(np.float32))
 
 
 def dot(a, b, precision=lax.Precision.HIGHEST):
@@ -61,6 +70,31 @@
 
 def dot_nt(a, b, precision=lax.Precision.HIGHEST):
     return lax.dot_general(a, b, (((1,), (1,)), ((), ())), precision=precision, preferred_element_type=F32)
+
+
+def parts_of(x):
+    parts = []
+    for _ in range(PARTS):
+        parts.append(x.astype(BF16))
+        x = x - parts[-1].astype(F32)
+    return parts
+
+
+def table_dot(table, x):
+    p = parts_of(x)
+    pair = jnp.concatenate(p[:2], 1)
+    top = dot(table[0], pair, None)
+    if PARTS == 2:
+        return top[:, :LANES] + (top[:, LANES:] + dot(table[1], p[0], None))
+    low = dot(table[1], pair, None)
+    last = dot(table[0], p[2], None) + dot(table[2], p[0], None)
+    return top[:, :LANES] + ((top[:, LANES:] + low[:, :LANES]) + (low[:, LANES:] + last))
+
+
+def dot_table(x, table):
+    p = parts_of(x)
+    pairs = [(i, k - i) for k in reversed(range(PARTS)) for i in range(k + 1)]
+    return functools.reduce(jnp.add, [dot(p[i], table[j], None) for i, j in pairs])
 
 
 def inverse_factor(gram):
@@ -244,6 +278,8 @@
         [jnp.where(lane_ids == low[r : r + 1], 1.0, 0.0).astype(BF16) for r in range(8)], 1
     )
     count_send[...] = dot_nt(high_hot[...], hits, None)
+    to_lags(COUNTS, lambda p: count_send.at[rows_of(p)], count_recv.at[me])
+    drain(COUNTS, count_recv.at[pl.ds(0, N_LAG - 1)])
     count_recv[me] = count_send[rows_of(me), :]
 
     wait(recv_sems, SNAPS, snap_recv.at[pl.ds(0, N_LAG - 1)])
@@ -258,19 +294,6 @@
     to_lags(CORR, lambda p: corr_send.at[rows_of(p)], corr_recv.at[me])
     drain(CORR, corr_recv.at[pl.ds(0, N_LAG - 1)])
     corr_recv[me] = corr_send[rows_of(me), :]
-    to_lags(COUNTS, lambda p: count_send.at[rows_of(p)], count_recv.at[me])
-    drain(COUNTS, count_recv.at[pl.ds(0, N_LAG - 1)])
-    for k in range(OWN):
-        j = lax.rem(own_col + k, OWN)
-        owner = (8 * j) // 3
-        pl.when(owner != me)(functools.partial(send, COLS, col_send.at[j], col_recv.at[me], "lag", owner))
-    drain(COLS, col_recv.at[pl.ds(0, OWN - 1)], active)
-    drain(COLS, col_recv.at[pl.ds(0, OWN)], idle)
-
-    @pl.when(active)
-    def _():
-        col_recv[me] = col_send[own_col]
-
     wait(recv_sems, LIVE, live_recv.at[pl.ds(0, N_SNAP - 1)])
     total = jnp.sum(live_recv[...], axis=0)
 
@@ -297,6 +320,17 @@
     to_lags(BINS, lambda p: bin_send.at[rows_of(p)], bin_recv.at[me])
     drain(BINS, bin_recv.at[pl.ds(0, N_LAG - 1)])
     bin_recv[me] = bin_send[rows_of(me), :]
+    for k in range(OWN):
+        j = lax.rem(own_col + k, OWN)
+        owner = (8 * j) // 3
+        pl.when(owner != me)(functools.partial(send, COLS, col_send.at[j], col_recv.at[me], "lag", owner))
+    drain(COLS, col_recv.at[pl.ds(0, OWN - 1)], active)
+    drain(COLS, col_recv.at[pl.ds(0, OWN)], idle)
+
+    @pl.when(active)
+    def _():
+        col_recv[me] = col_send[own_col]
+
     wait(recv_sems, COUNTS, count_recv.at[pl.ds(0, N_LAG - 1)])
     divisor = jnp.maximum(jnp.sum(count_recv[...], axis=0), 1.0) * total
     wait(recv_sems, BINS, bin_recv.at[pl.ds(0, N_LAG - 1)])
@@ -313,16 +347,16 @@
         load.wait()
 
     def rising(v):
-        a = dot(forward[...], v)
+        a = table_dot(forward, v)
         ar, ai = a[:FIRST], a[FIRST:]
         tc, ts = twists[0], twists[1]
         return jnp.concatenate([ar * tc + ai * ts, ai * tc - ar * ts], 1)
 
     def apply(v, spectrum):
-        e = dot(dot(rising(v), across[...]) * spectrum, back[...])
+        e = dot_table(dot_table(rising(v), across) * spectrum, back)
         er, ei = e[:, :LANES], e[:, LANES:]
         tc, ts = twists[0], twists[1]
-        return dot(backward[...], jnp.concatenate([er * tc - ei * ts, ei * tc + er * ts], 0))
+        return table_dot(backward, jnp.concatenate([er * tc - ei * ts, ei * tc + er * ts], 0))
 
     pl.when(active)(lambda: wait(recv_sems, COLS, col_recv.at[pl.ds(0, N_LAG - 1)]))
     column = jnp.where(active, col_recv[...].reshape(2 * HALF, LANES), 0.0)
@@ -331,7 +365,7 @@
     whole = lag_recv[...].reshape(2 * HALF, LANES)
     ids = [lax.broadcasted_iota(jnp.int32, (2 * HALF, LANES), d) for d in range(2)]
     whole = jnp.where((ids[0] == 0) & (ids[1] == 0), 0.5 * whole, whole)
-    half_spectrum = dot(rising(whole), across[:, :LANES]) * (2.0 / PADDED)
+    half_spectrum = dot_table(rising(whole), across.at[:, :, :LANES]) * (2.0 / PADDED)
     spectrum = jnp.concatenate([half_spectrum, half_spectrum], 1)
 
     for sweep in range(ITERS):
@@ -348,17 +382,22 @@
 
         drain(IMAGE + 4 * sweep, image_send.at[sweep, pl.ds(0, 2 * HALF - 8)], active)
 
+    images_in = []
     for sweep in range(ITERS):
         group = image_all.at[sweep, pl.ds(block * OWN, OWN)]
         some, every = (image_all.at[sweep, pl.ds(0, n)] for n in (OWN - 1, OWN))
         pl.when(active)(functools.partial(wait, recv_sems, IMAGE + 4 * sweep, some))
         pl.when(idle)(functools.partial(wait, recv_sems, IMAGE + 4 * sweep, every))
-        to_snaps(IMAGE_ALL + 4 * sweep, group, group)
-        drain(IMAGE_ALL + 4 * sweep, image_all.at[sweep, pl.ds(0, COLUMNS - OWN)])
+        reach = N_SNAP // 2 if sweep == 0 else N_SNAP - 1
+        for d in far_first(N_SNAP):
+            if N_SNAP - d <= reach:
+                send(IMAGE_ALL + 4 * sweep, group, group, "snap", lax.rem(block + d, N_SNAP))
+        images_in.append(image_all.at[sweep, pl.ds(0, reach * OWN)])
+        drain(IMAGE_ALL + 4 * sweep, images_in[sweep])
 
     images = []
     for sweep in range(ITERS):
-        wait(recv_sems, IMAGE_ALL + 4 * sweep, image_all.at[sweep, pl.ds(0, COLUMNS - OWN)])
+        wait(recv_sems, IMAGE_ALL + 4 * sweep, images_in[sweep])
         image = jnp.concatenate([image_all[sweep, :, i, :] for i in range(2 * PER)], 1)
         own = jnp.concatenate(
             [image_all[sweep, pl.ds(block * OWN, OWN), i, :] for i in range(2 * PER)], 1
@@ -381,7 +420,14 @@
         wait(recv_sems, GRAM_ALL + 4 * sweep, gram_all.at[sweep, pl.ds(0, N_SNAP - 1)])
         for s in range(N_SNAP):
             gram_full[sweep, s * OWN : (s + 1) * OWN, :] = gram_all[sweep, s]
-        return gram_full[sweep]
+        if sweep:
+            return gram_full[sweep]
+        known, spots = gram_full[sweep], (COLUMNS, LANES)
+        row_block = lax.broadcasted_iota(jnp.int32, spots, 0) // OWN
+        col_block = lax.broadcasted_iota(jnp.int32, spots, 1) // OWN
+        own = (col_block + N_SNAP - row_block) % N_SNAP <= N_SNAP // 2
+        square = jnp.concatenate([known, jnp.zeros((LANES - COLUMNS, LANES), F32)], 0)
+        return jnp.where(own, known, square.T[:COLUMNS])
 
     inverse = inverse_factor(whole_gram(0))[:, :COLUMNS]
     mapped = dot(inverse, images[1])
@@ -440,7 +486,7 @@
             pltpu.SemaphoreType.DMA((len(operands),)),
         ],
         compiler_params=pltpu.CompilerParams(
-            collective_id=0, has_side_effects=True, vmem_limit_bytes=48 << 20
+            collective_id=0, has_side_effects=True, vmem_limit_bytes=56 << 20
         ),
         name="coarray_subspace",
     )(counts, *operands)

time: 93.7 us -> 85.4 us (0.911)
  local copies, waits for them, and re-layouts: 8.84 us -> 3.03 us
  Pallas kernels: 83.2 us -> 81 us
    unnamed x18 -> x2, local copies, waits for them, and re-layouts: 8.84 us -> 3.03 us
    pallas_call x1, Pallas kernels: 83.2 us -> 81 us  [on_device(): pl.pallas_call(kernel, out_shape=(jax.ShapeDtypeStruct((2, PER * LANES),...]
where the time goes in v2:
time: 85.4 us; the launch traced here: 85.3 us
  Pallas kernels  81 us (95%)
  local copies, waits for them, and re-layouts  3.03 us (4%)
  between operations  1.29 us (2%)
    pallas_call x1, Pallas kernels, on_device(): pl.pallas_call(kernel, out_shape=(jax.ShapeDtypeStruct((2, PER * LANES),...  81 us
    unnamed x2, local copies, waits for them, and re-layouts  3.03 us

profile of v2, /device:TPU:1, one launch (start us, length us, event | category | flops | bytes accessed | tf_op | source)
XLA Modules:
  0.0 85.3 jit_solution(11438870611488211691)
XLA Ops:
  1.3 81.0 %coarray_subspace.1 = (f32[2,512]{1,0:T(2,128)}, f32[2,96,512]{2,1,0:T(8,128)}) custom-call(s32[1]{0:T(128)S(6)} %copy.13.counts, s32[1,256]{1,0:T(1,128)} %bitcast.3, bf16[2,8,4096]{2,1,0:T(8,128)(2,1)} %bitcast.2, f32[2,96,512]{2,1,0:T(8,128)} %initial_in.1, bf16[3,512,256]{2,1,0:T(8,128)(2,1)} %constant.10.clone.forward_in, ...), custom_call_target="tpu_custom_call" | custom-call | tf_op jit(solution)/shard_map/coarray_subspace/pallas_call | solution.py:449
  82.3 1.3 %copy.14 = f32[2,512]{1,0:T(2,128)} copy(f32[2,512]{1,0:T(2,128)} %get-tuple-element.4) | data formatting | bytes 8192
  83.5 1.8 %copy.15 = f32[2,96,512]{2,1,0:T(8,128)} copy(f32[2,96,512]{2,1,0:T(8,128)} %get-tuple-element.5) | data formatting | bytes 786432

commit v3 on v2

--- a/solution.py
+++ b/solution.py
@@ -31,7 +31,7 @@
 SNAPS, CORR, CORR_ALL, BINS, LAGCORR, COLS, COUNTS, LIVE = range(8)
 IMAGE, IMAGE_ALL, GRAM, GRAM_ALL = range(8, 12)
 PHASES = 8 + 4 * ITERS
-BLOCK = 4
+BLOCK = 8
 PARTS = 3
 
 
@@ -107,17 +107,16 @@
     def spread(x):
         return jnp.broadcast_to(x, shape)
 
-    for start in range(0, COLUMNS, BLOCK):
-        t, first = divmod(start, 8)
+    for t in range(COLUMNS // BLOCK):
+        start = BLOCK * t
         own = tiles[t]
         inside = (lane >= start) & (lane < start + BLOCK)
         s = [
-            [spread(own[first + k : first + k + 1, start + m : start + m + 1]) for m in range(k + 1)]
-            for k in range(BLOCK)
+            [spread(own[k : k + 1, start + m : start + m + 1]) for m in range(k + 1)] for k in range(BLOCK)
         ]
         rows = []
         for k in range(BLOCK):
-            row = jnp.where(inside, 0.0, spread(own[first + k : first + k + 1, :]))
+            row = jnp.where(inside, 0.0, spread(own[k : k + 1, :]))
             rows.append(jnp.where(lane == start + k, 1.0, row))
         inverses = []
         for m in range(BLOCK):
@@ -127,9 +126,7 @@
                 for n in range(m + 1, k + 1):
                     s[k][n] = s[k][n] - factors[k] * s[n][m]
                 rows[k] = rows[k] - factors[k] * rows[m]
-        for u in range(t, len(tiles)):
-            if u == t and first + BLOCK == 8:
-                continue
+        for u in range(t + 1, len(tiles)):
             rest = jnp.where(inside, 0.0, tiles[u])
             cols = [spread(tiles[u][:, start + m : start + m + 1]) for m in range(BLOCK)]
             for m in range(BLOCK):
@@ -138,14 +135,9 @@
                     cols[n] = cols[n] - multiplier * s[n][m]
                 rest = rest - multiplier * rows[m]
             tiles[u] = rest
-        if first + BLOCK == 8:
-            kept = own
-        else:
-            kept = jnp.where(sub < first, own, tiles[t])
         for k in range(BLOCK):
-            kept = jnp.where(sub == first + k, rows[k], kept)
-            pivots[t] = jnp.where(sub == first + k, s[k][k], pivots[t])
-        tiles[t] = kept
+            tiles[t] = rows[k] if k == 0 else jnp.where(sub == k, rows[k], tiles[t])
+            pivots[t] = jnp.where(sub == k, s[k][k], pivots[t])
     return jnp.concatenate(
         [
             jnp.where(lane <= 8 * t + sub, tile, 0.0) * (1.0 / jnp.sqrt(pivots[t]))
@@ -161,7 +153,7 @@
 
 def kernel(
     counts, positions_in, snaps_in, initial_in, forward_in, across_in, back_in, backward_in, twists_in,
-    lag_out, sub_out,
+    lag_out, inverse_out, mapped_out,
     positions, snaps, initial, forward, across, back, backward, twists,
     snap_send, snap_recv, corr_send, corr_recv, row_send, row_recv, bin_send, bin_recv,
     count_send, count_recv, live_send, live_recv, high_hot,
@@ -187,8 +179,6 @@
             ]
         )
     ]
-    for load in loads:
-        load.start()
 
     def all_lags(act):
         for z, y in shifts:
@@ -230,6 +220,9 @@
     barrier = pltpu.get_barrier_semaphore()
     all_lags(lambda p: pl.semaphore_signal(barrier, inc=1, device_id={"lag": p}, device_id_type=MESH))
     all_snaps(lambda p: pl.semaphore_signal(barrier, inc=1, device_id={"snap": p}, device_id_type=MESH))
+
+    for load in loads:
+        load.start()
 
     loads[0].wait()
     live = lax.broadcasted_iota(jnp.int32, (8, ROWS), 1) < counts[0]
@@ -339,9 +332,7 @@
     to_lags(LAGCORR, lambda p: lag_send, lag_recv.at[me])
     drain(LAGCORR, lag_recv.at[pl.ds(0, N_LAG - 1)])
     lag_recv[me] = lag_corr
-    for c in range(2):
-        for r in range(PER):
-            lag_out[c : c + 1, r * LANES : (r + 1) * LANES] = lag_corr[c * PER + r : c * PER + r + 1, :]
+    lag_out[...] = lag_corr
 
     for load in loads[3:]:
         load.wait()
@@ -430,31 +421,40 @@
         return jnp.where(own, known, square.T[:COLUMNS])
 
     inverse = inverse_factor(whole_gram(0))[:, :COLUMNS]
-    mapped = dot(inverse, images[1])
+    mapped_out[...] = dot(inverse, images[1])
     gram = dot_nt(dot(inverse, whole_gram(1)[:, :COLUMNS]), inverse)
     gram = jnp.concatenate([gram, jnp.zeros((COLUMNS, LANES - COLUMNS), F32)], 1)
-    result = dot(inverse_factor(gram)[:, :COLUMNS], mapped)
+    inverse_out[...] = inverse_factor(gram)
+
+    for finish in drains:
+        finish()
+
+
+def combine(lag_corr, inverse, mapped, lag_out, sub_out):
+    for c in range(2):
+        for r in range(PER):
+            row = c * PER + r
+            lag_out[c : c + 1, r * LANES : (r + 1) * LANES] = lag_corr[row : row + 1, :]
+    result = dot(inverse[:, :COLUMNS], mapped[...])
     for c in range(2):
         sub_out[c] = result[:, c * PER * LANES : (c + 1) * PER * LANES]
 
-    for finish in drains:
-        finish()
-
 
 def on_device(snapshots, positions, counts, initial):
     constants = [jnp.asarray(t) for t in tables()]
-    operands = (positions.reshape(1, SENSORS), jnp.transpose(snapshots, (0, 2, 1)), initial, *constants)
+    operands = tuple(pltpu.with_memory_space_constraint(a, pltpu.HBM) for a in (positions.reshape(1, SENSORS), jnp.transpose(snapshots, (0, 2, 1)), initial, *constants))
     vmem = pl.BlockSpec(memory_space=pltpu.VMEM)
     tile = (2 * PER, LANES)
-    return pl.pallas_call(
+    pieces = pl.pallas_call(
         kernel,
         out_shape=(
-            jax.ShapeDtypeStruct((2, PER * LANES), F32),
-            jax.ShapeDtypeStruct((2, COLUMNS, PER * LANES), F32),
+            jax.ShapeDtypeStruct(tile, F32),
+            jax.ShapeDtypeStruct((COLUMNS, LANES), F32),
+            jax.ShapeDtypeStruct((COLUMNS, 2 * PER * LANES), F32),
         ),
         in_specs=[pl.BlockSpec(memory_space=pltpu.SMEM)]
         + [pl.BlockSpec(memory_space=pltpu.HBM)] * len(operands),
-        out_specs=(vmem, vmem),
+        out_specs=(vmem, vmem, vmem),
         scratch_shapes=[pltpu.VMEM(a.shape, a.dtype) for a in operands]
         + [
             pltpu.VMEM((2, 8, ROWS), BF16),
@@ -486,10 +486,21 @@
             pltpu.SemaphoreType.DMA((len(operands),)),
         ],
         compiler_params=pltpu.CompilerParams(
-            collective_id=0, has_side_effects=True, vmem_limit_bytes=56 << 20
+            collective_id=0, has_side_effects=True, vmem_limit_bytes=24 << 20
         ),
         name="coarray_subspace",
     )(counts, *operands)
+    return pl.pallas_call(
+        combine,
+        out_shape=(
+            jax.ShapeDtypeStruct((2, PER * LANES), F32),
+            jax.ShapeDtypeStruct((2, COLUMNS, PER * LANES), F32),
+        ),
+        in_specs=[vmem] * 3,
+        out_specs=(vmem, vmem),
+        compiler_params=pltpu.CompilerParams(vmem_limit_bytes=4 << 20),
+        name="combine_columns",
+    )(*pieces)
 
 
 def solution(mesh):

time: 85.4 us -> 80 us (0.937)
  local copies, waits for them, and re-layouts: 3.03 us -> 0 us
  Pallas kernels: 81 us -> 78.6 us
    unnamed x2 -> x0, local copies, waits for them, and re-layouts: 3.03 us -> none
    pallas_call x1 -> x2, Pallas kernels: 81 us -> 78.6 us  [the longest x1 77.4 us: on_device(): pl.pallas_call(kernel, out_shape=(jax.ShapeDtypeStruct(tile, F32), jax.Sh...]
where the time goes in v3:
time: 80 us; the launch traced here: 79.9 us
  Pallas kernels  78.6 us (98%)
  between operations  1.28 us (2%)
    pallas_call x1, Pallas kernels, on_device(): pl.pallas_call(kernel, out_shape=(jax.ShapeDtypeStruct(tile, F32), jax.Sh...  77.4 us

profile of v3, /device:TPU:1, one launch (start us, length us, event | category | flops | bytes accessed | tf_op | source)
XLA Modules:
  0.0 79.9 jit_solution(9598075239133348524)
XLA Ops:
  1.3 77.4 %coarray_subspace.1 = (f32[8,128]{1,0:T(8,128)S(1)}, f32[96,128]{1,0:T(8,128)S(1)}, f32[96,1024]{1,0:T(8,128)S(1)}) custom-call(s32[1]{0:T(128)S(6)} %copy.11.counts, s32[1,256]{1,0:T(1,128)} %bitcast.3, bf16[2,8,4096]{2,1,0:T(8,128)(2,1)} %bitcast.2, f32[2,96,512]{2,1,0:T(8,128)} %initial_in.1, bf16[3,512,256]{2,1,0:T(8,128)(2,1)} %constant.10.clone.forward_in, ...), custom_call_target="tpu_custom_call" | custom-call | tf_op jit(solution)/shard_map/coarray_subspace/pallas_call | solution.py:448
  78.7 1.2 %combine_columns.1 = (f32[2,512]{1,0:T(2,128)}, f32[2,96,512]{2,1,0:T(8,128)}) custom-call(f32[8,128]{1,0:T(8,128)S(1)} %get-tuple-element.5.lag_corr, f32[96,128]{1,0:T(8,128)S(1)} %get-tuple-element.6.inverse, f32[96,1024]{1,0:T(8,128)S(1)} %get-tuple-element.7.mapped), custom_call_target="tpu_custom_call" | custom-call | tf_op jit(solution)/shard_map/combine_columns/pallas_call | solution.py:493

commit v4 on v3

--- a/solution.py
+++ b/solution.py
@@ -28,9 +28,11 @@
 HALF = LAGS // LANES
 PER = HALF // N_LAG
 
-SNAPS, CORR, CORR_ALL, BINS, LAGCORR, COLS, COUNTS, LIVE = range(8)
-IMAGE, IMAGE_ALL, GRAM, GRAM_ALL = range(8, 12)
-PHASES = 8 + 4 * ITERS
+SNAPS, CORR, CORR_ALL, BINS, LAGCORR, COLS, COUNTS, LIVE, PAIR, REST = range(10)
+IMAGE, IMAGE_ALL, GRAM, GRAM_ALL = range(10, 14)
+PHASES = 10 + 4 * ITERS
+REACH = N_SNAP // 2
+NEAR = (REACH + 1) * OWN
 BLOCK = 8
 PARTS = 3
 
@@ -155,7 +157,7 @@
     counts, positions_in, snaps_in, initial_in, forward_in, across_in, back_in, backward_in, twists_in,
     lag_out, inverse_out, mapped_out,
     positions, snaps, initial, forward, across, back, backward, twists,
-    snap_send, snap_recv, corr_send, corr_recv, row_send, row_recv, bin_send, bin_recv,
+    snap_send, snap_recv, corr_half, pair_recv, corr_send, corr_recv, row_send, row_recv, bin_send, bin_recv,
     count_send, count_recv, live_send, live_recv, high_hot,
     lag_send, lag_recv, col_send, col_recv, image_send, image_all, gram_send, gram_recv,
     strip_send, gram_all, gram_full,
@@ -283,7 +285,14 @@
     imag = dot_nt(turned, left, None)
     square = (SENSORS, SENSORS)
     below = lax.broadcasted_iota(jnp.int32, square, 0) >= lax.broadcasted_iota(jnp.int32, square, 1)
-    corr_send[...] = jnp.where(below, real, imag)
+    packed = jnp.where(below, real, imag)
+    for c in range(2):
+        corr_half[c] = packed[:, c * LANES : (c + 1) * LANES]
+    core = lax.rem(block, 2)
+    send(PAIR, corr_half.at[1 - core], pair_recv, "snap", block + 1 - 2 * core)
+    drain(PAIR, pair_recv)
+    wait(recv_sems, PAIR, pair_recv)
+    corr_send[...] = corr_half[core] + pair_recv[...]
     to_lags(CORR, lambda p: corr_send.at[rows_of(p)], corr_recv.at[me])
     drain(CORR, corr_recv.at[pl.ds(0, N_LAG - 1)])
     corr_recv[me] = corr_send[rows_of(me), :]
@@ -296,7 +305,8 @@
     drain(CORR_ALL, row_recv.at[pl.ds(0, N_SNAP - 1)])
     row_recv[block] = row_send[...]
     wait(recv_sems, CORR_ALL, row_recv.at[pl.ds(0, N_SNAP - 1)])
-    values = jnp.sum(row_recv[...], axis=0) * sign
+    halves = [sum(row_recv[2 * x + c] for x in range(N_SNAP // 2)) for c in range(2)]
+    values = jnp.concatenate(halves, 1) * sign
     part_0 = values.astype(BF16).astype(F32)
     part_1 = (values - part_0).astype(BF16).astype(F32)
     part_2 = values - part_0 - part_1
@@ -373,32 +383,40 @@
 
         drain(IMAGE + 4 * sweep, image_send.at[sweep, pl.ds(0, 2 * HALF - 8)], active)
 
-    images_in = []
+    def to_blocks(phase, sweep, ahead):
+        group = image_all.at[sweep, pl.ds(block * OWN, OWN)]
+        for d in far_first(N_SNAP):
+            if N_SNAP - d in ahead:
+                send(phase, group, group, "snap", lax.rem(block + d, N_SNAP))
+        landed = image_all.at[sweep, pl.ds(0, len(ahead) * OWN)]
+        drain(phase, landed)
+        return landed
+
+    near = []
     for sweep in range(ITERS):
-        group = image_all.at[sweep, pl.ds(block * OWN, OWN)]
         some, every = (image_all.at[sweep, pl.ds(0, n)] for n in (OWN - 1, OWN))
         pl.when(active)(functools.partial(wait, recv_sems, IMAGE + 4 * sweep, some))
         pl.when(idle)(functools.partial(wait, recv_sems, IMAGE + 4 * sweep, every))
-        reach = N_SNAP // 2 if sweep == 0 else N_SNAP - 1
-        for d in far_first(N_SNAP):
-            if N_SNAP - d <= reach:
-                send(IMAGE_ALL + 4 * sweep, group, group, "snap", lax.rem(block + d, N_SNAP))
-        images_in.append(image_all.at[sweep, pl.ds(0, reach * OWN)])
-        drain(IMAGE_ALL + 4 * sweep, images_in[sweep])
-
-    images = []
+        near.append(to_blocks(IMAGE_ALL + 4 * sweep, sweep, range(1, REACH + 1)))
+
+    def rows_from(sweep, start, size):
+        return jnp.concatenate(
+            [image_all[sweep, pl.ds(start, size), i, :] for i in range(2 * PER)], 1
+        )
+
     for sweep in range(ITERS):
-        wait(recv_sems, IMAGE_ALL + 4 * sweep, images_in[sweep])
-        image = jnp.concatenate([image_all[sweep, :, i, :] for i in range(2 * PER)], 1)
-        own = jnp.concatenate(
-            [image_all[sweep, pl.ds(block * OWN, OWN), i, :] for i in range(2 * PER)], 1
-        )
-        images.append(image)
-        gram_send[sweep, :, :COLUMNS] = dot_nt(own, image) * (1.0 / LAGS)
-        gram_send[sweep, :, COLUMNS:] = jnp.zeros((OWN, LANES - COLUMNS), F32)
+        wait(recv_sems, IMAGE_ALL + 4 * sweep, near[sweep])
+        blocks = [
+            rows_from(sweep, lax.rem(block + d, N_SNAP) * OWN, OWN) for d in range(REACH + 1)
+        ]
+        strip = dot_nt(blocks[0], jnp.concatenate(blocks, 0)) * (1.0 / LAGS)
+        strip = jnp.concatenate([strip, jnp.zeros((OWN, LANES // 2 - NEAR), F32)], 1)
+        gram_send[sweep, : OWN // 2, :] = jnp.concatenate([strip[: OWN // 2], strip[OWN // 2 :]], 1)
+        gram_send[sweep, OWN // 2 :, :] = jnp.zeros((8 - OWN // 2, LANES), F32)
         to_lags(GRAM + 4 * sweep, lambda p: gram_send.at[sweep], gram_recv.at[sweep, me])
         drain(GRAM + 4 * sweep, gram_recv.at[sweep, pl.ds(0, N_LAG - 1)])
         gram_recv[sweep, me] = gram_send[sweep]
+    rest = to_blocks(REST, ITERS - 1, range(REACH + 1, N_SNAP))
 
     for sweep in range(ITERS):
         wait(recv_sems, GRAM + 4 * sweep, gram_recv.at[sweep, pl.ds(0, N_LAG - 1)])
@@ -410,20 +428,25 @@
     def whole_gram(sweep):
         wait(recv_sems, GRAM_ALL + 4 * sweep, gram_all.at[sweep, pl.ds(0, N_SNAP - 1)])
         for s in range(N_SNAP):
-            gram_full[sweep, s * OWN : (s + 1) * OWN, :] = gram_all[sweep, s]
-        if sweep:
-            return gram_full[sweep]
+            tile = gram_all[sweep, s]
+            strip = jnp.concatenate([tile[: OWN // 2, :NEAR], tile[: OWN // 2, LANES // 2 : LANES // 2 + NEAR]], 0)
+            first = s * OWN
+            fits = min(NEAR, COLUMNS - first)
+            gram_full[sweep, first : first + OWN, first : first + fits] = strip[:, :fits]
+            if fits < NEAR:
+                gram_full[sweep, first : first + OWN, : NEAR - fits] = strip[:, fits:]
         known, spots = gram_full[sweep], (COLUMNS, LANES)
         row_block = lax.broadcasted_iota(jnp.int32, spots, 0) // OWN
-        col_block = lax.broadcasted_iota(jnp.int32, spots, 1) // OWN
-        own = (col_block + N_SNAP - row_block) % N_SNAP <= N_SNAP // 2
+        lane = lax.broadcasted_iota(jnp.int32, spots, 1)
+        ahead = (lane // OWN + N_SNAP - row_block) % N_SNAP
         square = jnp.concatenate([known, jnp.zeros((LANES - COLUMNS, LANES), F32)], 0)
-        return jnp.where(own, known, square.T[:COLUMNS])
+        return jnp.where(lane >= COLUMNS, 0.0, jnp.where(ahead <= REACH, known, square.T[:COLUMNS]))
 
     inverse = inverse_factor(whole_gram(0))[:, :COLUMNS]
-    mapped_out[...] = dot(inverse, images[1])
     gram = dot_nt(dot(inverse, whole_gram(1)[:, :COLUMNS]), inverse)
     gram = jnp.concatenate([gram, jnp.zeros((COLUMNS, LANES - COLUMNS), F32)], 1)
+    wait(recv_sems, REST, rest)
+    mapped_out[...] = dot(inverse, rows_from(ITERS - 1, 0, COLUMNS))
     inverse_out[...] = inverse_factor(gram)
 
     for finish in drains:
@@ -459,10 +482,12 @@
         + [
             pltpu.VMEM((2, 8, ROWS), BF16),
             pltpu.VMEM((N_LAG, 2, 8, LANES), BF16),
-            pltpu.VMEM((SENSORS, SENSORS), F32),
-            pltpu.VMEM((N_LAG, 8, SENSORS), F32),
-            pltpu.VMEM((8, SENSORS), F32),
-            pltpu.VMEM((N_SNAP, 8, SENSORS), F32),
+            pltpu.VMEM((2, SENSORS, LANES), F32),
+            pltpu.VMEM((SENSORS, LANES), F32),
+            pltpu.VMEM((SENSORS, LANES), F32),
+            pltpu.VMEM((N_LAG, 8, LANES), F32),
+            pltpu.VMEM((8, LANES), F32),
+            pltpu.VMEM((N_SNAP, 8, LANES), F32),
             pltpu.VMEM((2 * HALF, LANES), F32),
             pltpu.VMEM((N_LAG, *tile), F32),
             pltpu.VMEM((2 * HALF, LANES), F32),
@@ -476,10 +501,10 @@
             pltpu.VMEM((N_LAG, *tile), F32),
             pltpu.VMEM((ITERS, 2 * HALF, LANES), F32),
             pltpu.VMEM((ITERS, COLUMNS, *tile), F32),
-            pltpu.VMEM((ITERS, OWN, LANES), F32),
-            pltpu.VMEM((ITERS, N_LAG, OWN, LANES), F32),
-            pltpu.VMEM((ITERS, OWN, LANES), F32),
-            pltpu.VMEM((ITERS, N_SNAP, OWN, LANES), F32),
+            pltpu.VMEM((ITERS, 8, LANES), F32),
+            pltpu.VMEM((ITERS, N_LAG, 8, LANES), F32),
+            pltpu.VMEM((ITERS, 8, LANES), F32),
+            pltpu.VMEM((ITERS, N_SNAP, 8, LANES), F32),
             pltpu.VMEM((ITERS, COLUMNS, LANES), F32),
             pltpu.SemaphoreType.DMA((PHASES,)),
             pltpu.SemaphoreType.DMA((PHASES,)),

time: 80 us -> 77 us (0.963)
  Pallas kernels: 78.6 us -> 75.7 us
    pallas_call x1, Pallas kernels: 77.4 us -> 74.5 us  [on_device(): pl.pallas_call(kernel, out_shape=(jax.ShapeDtypeStruct(tile, F32), jax.Sh...]
where the time goes in v4:
time: 77 us
  Pallas kernels  75.7 us (98%)
  between operations  1.28 us (2%)
    pallas_call x1, Pallas kernels, on_device(): pl.pallas_call(kernel, out_shape=(jax.ShapeDtypeStruct(tile, F32), jax.Sh...  74.5 us

profile of v4, /device:TPU:1, one launch (start us, length us, event | category | flops | bytes accessed | tf_op | source)
XLA Modules:
  0.0 77.0 jit_solution(13593317340135144793)
XLA Ops:
  1.3 74.5 %coarray_subspace.1 = (f32[8,128]{1,0:T(8,128)S(1)}, f32[96,128]{1,0:T(8,128)S(1)}, f32[96,1024]{1,0:T(8,128)S(1)}) custom-call(s32[1]{0:T(128)S(6)} %copy.11.counts, s32[1,256]{1,0:T(1,128)} %bitcast.3, bf16[2,8,4096]{2,1,0:T(8,128)(2,1)} %bitcast.2, f32[2,96,512]{2,1,0:T(8,128)} %initial_in.1, bf16[3,512,256]{2,1,0:T(8,128)(2,1)} %constant.10.clone.forward_in, ...), custom_call_target="tpu_custom_call" | custom-call | tf_op jit(solution)/shard_map/coarray_subspace/pallas_call | solution.py:471
  75.7 1.2 %combine_columns.1 = (f32[2,512]{1,0:T(2,128)}, f32[2,96,512]{2,1,0:T(8,128)}) custom-call(f32[8,128]{1,0:T(8,128)S(1)} %get-tuple-element.5.lag_corr, f32[96,128]{1,0:T(8,128)S(1)} %get-tuple-element.6.inverse, f32[96,1024]{1,0:T(8,128)S(1)} %get-tuple-element.7.mapped), custom_call_target="tpu_custom_call" | custom-call | tf_op jit(solution)/shard_map/combine_columns/pallas_call | solution.py:518

commit v5 on v4

--- a/solution.py
+++ b/solution.py
@@ -34,7 +34,7 @@
 REACH = N_SNAP // 2
 NEAR = (REACH + 1) * OWN
 BLOCK = 8
-PARTS = 3
+PARTS = 2
 
 
 def tables():
@@ -158,7 +158,7 @@
     lag_out, inverse_out, mapped_out,
     positions, snaps, initial, forward, across, back, backward, twists,
     snap_send, snap_recv, corr_half, pair_recv, corr_send, corr_recv, row_send, row_recv, bin_send, bin_recv,
-    count_send, count_recv, live_send, live_recv, high_hot,
+    started, count_send, count_recv, live_send, live_recv, high_hot,
     lag_send, lag_recv, col_send, col_recv, image_send, image_all, gram_send, gram_recv,
     strip_send, gram_all, gram_full,
     send_sems, recv_sems, load_sems,
@@ -239,17 +239,6 @@
             col_send[:, c * PER + r, :] = jnp.where(odd, pair[OWN:], pair[:OWN])
     live_send[...] = jnp.full((8, LANES), counts[0].astype(F32), F32)
     live_recv[block] = live_send[...]
-    pl.semaphore_wait(barrier, N_LAG + N_SNAP - 2)
-
-    def snap_piece(p):
-        return snap_send.at[:, :, pl.ds(pl.multiple_of(p * LANES, LANES), LANES)]
-
-    to_lags(SNAPS, snap_piece, snap_recv.at[me])
-    drain(SNAPS, snap_recv.at[pl.ds(0, N_LAG - 1)])
-    snap_recv[me] = snap_send[:, :, pl.ds(pl.multiple_of(me * LANES, LANES), LANES)]
-    to_snaps(LIVE, live_send, live_recv.at[block])
-    drain(LIVE, live_recv.at[pl.ds(0, N_SNAP - 1)])
-
     loads[2].wait()
     strip = (8, SENSORS)
     sensor = me * 8 + lax.broadcasted_iota(jnp.int32, strip, 0)
@@ -273,8 +262,17 @@
         [jnp.where(lane_ids == low[r : r + 1], 1.0, 0.0).astype(BF16) for r in range(8)], 1
     )
     count_send[...] = dot_nt(high_hot[...], hits, None)
-    to_lags(COUNTS, lambda p: count_send.at[rows_of(p)], count_recv.at[me])
-    drain(COUNTS, count_recv.at[pl.ds(0, N_LAG - 1)])
+    pl.semaphore_wait(barrier, N_LAG + N_SNAP - 2)
+
+    def snap_piece(p):
+        return snap_send.at[:, :, pl.ds(pl.multiple_of(p * LANES, LANES), LANES)]
+
+    to_lags(SNAPS, snap_piece, snap_recv.at[me])
+    drain(SNAPS, snap_recv.at[pl.ds(0, N_LAG - 1)])
+    snap_recv[me] = snap_send[:, :, pl.ds(pl.multiple_of(me * LANES, LANES), LANES)]
+    to_snaps(LIVE, live_send, live_recv.at[block])
+    drain(LIVE, live_recv.at[pl.ds(0, N_SNAP - 1)])
+
     count_recv[me] = count_send[rows_of(me), :]
 
     wait(recv_sems, SNAPS, snap_recv.at[pl.ds(0, N_LAG - 1)])
@@ -303,6 +301,19 @@
     row_send[...] = jnp.sum(corr_recv[...], axis=0)
     to_snaps(CORR_ALL, row_send, row_recv.at[block])
     drain(CORR_ALL, row_recv.at[pl.ds(0, N_SNAP - 1)])
+    to_lags(COUNTS, lambda p: count_send.at[rows_of(p)], count_recv.at[me])
+    drain(COUNTS, count_recv.at[pl.ds(0, N_LAG - 1)])
+    for k in range(OWN):
+        j = lax.rem(own_col + k, OWN)
+        owner = (8 * j) // 3
+        pl.when(owner != me)(functools.partial(send, COLS, col_send.at[j], col_recv.at[me], "lag", owner))
+    drain(COLS, col_recv.at[pl.ds(0, OWN - 1)], active)
+    drain(COLS, col_recv.at[pl.ds(0, OWN)], idle)
+
+    @pl.when(active)
+    def _():
+        col_recv[me] = col_send[own_col]
+
     row_recv[block] = row_send[...]
     wait(recv_sems, CORR_ALL, row_recv.at[pl.ds(0, N_SNAP - 1)])
     halves = [sum(row_recv[2 * x + c] for x in range(N_SNAP // 2)) for c in range(2)]
@@ -323,17 +334,6 @@
     to_lags(BINS, lambda p: bin_send.at[rows_of(p)], bin_recv.at[me])
     drain(BINS, bin_recv.at[pl.ds(0, N_LAG - 1)])
     bin_recv[me] = bin_send[rows_of(me), :]
-    for k in range(OWN):
-        j = lax.rem(own_col + k, OWN)
-        owner = (8 * j) // 3
-        pl.when(owner != me)(functools.partial(send, COLS, col_send.at[j], col_recv.at[me], "lag", owner))
-    drain(COLS, col_recv.at[pl.ds(0, OWN - 1)], active)
-    drain(COLS, col_recv.at[pl.ds(0, OWN)], idle)
-
-    @pl.when(active)
-    def _():
-        col_recv[me] = col_send[own_col]
-
     wait(recv_sems, COUNTS, count_recv.at[pl.ds(0, N_LAG - 1)])
     divisor = jnp.maximum(jnp.sum(count_recv[...], axis=0), 1.0) * total
     wait(recv_sems, BINS, bin_recv.at[pl.ds(0, N_LAG - 1)])
@@ -353,14 +353,18 @@
         tc, ts = twists[0], twists[1]
         return jnp.concatenate([ar * tc + ai * ts, ai * tc - ar * ts], 1)
 
-    def apply(v, spectrum):
-        e = dot_table(dot_table(rising(v), across) * spectrum, back)
+    def transform(v):
+        return dot_table(rising(v), across)
+
+    def apply(transformed, spectrum):
+        e = dot_table(transformed * spectrum, back)
         er, ei = e[:, :LANES], e[:, LANES:]
         tc, ts = twists[0], twists[1]
         return table_dot(backward, jnp.concatenate([er * tc - ei * ts, ei * tc + er * ts], 0))
 
     pl.when(active)(lambda: wait(recv_sems, COLS, col_recv.at[pl.ds(0, N_LAG - 1)]))
     column = jnp.where(active, col_recv[...].reshape(2 * HALF, LANES), 0.0)
+    started[...] = transform(column)
 
     wait(recv_sems, LAGCORR, lag_recv.at[pl.ds(0, N_LAG - 1)])
     whole = lag_recv[...].reshape(2 * HALF, LANES)
@@ -369,10 +373,12 @@
     half_spectrum = dot_table(rising(whole), across.at[:, :, :LANES]) * (2.0 / PADDED)
     spectrum = jnp.concatenate([half_spectrum, half_spectrum], 1)
 
+    calm = spectrum * (1.0 / (jnp.max(jnp.abs(half_spectrum), keepdims=True) * PADDED))
     for sweep in range(ITERS):
         if sweep:
-            spectrum = spectrum * (1.0 / (jnp.max(jnp.abs(half_spectrum), keepdims=True) * PADDED))
-        column = apply(column, spectrum)
+            column = apply(transform(column), calm)
+        else:
+            column = apply(started[...], spectrum)
         image_send[sweep] = column
         slot = image_all.at[sweep, block * OWN + own_col]
 
@@ -490,6 +496,7 @@
             pltpu.VMEM((N_SNAP, 8, LANES), F32),
             pltpu.VMEM((2 * HALF, LANES), F32),
             pltpu.VMEM((N_LAG, *tile), F32),
+            pltpu.VMEM((FIRST, 2 * LANES), F32),
             pltpu.VMEM((2 * HALF, LANES), F32),
             pltpu.VMEM((N_LAG, *tile), F32),
             pltpu.VMEM((8, LANES), F32),

time: 77 us -> 74.7 us (0.970)
  Pallas kernels: 75.7 us -> 73.4 us
    pallas_call x1, Pallas kernels: 74.5 us -> 72.1 us  [on_device(): pl.pallas_call(kernel, out_shape=(jax.ShapeDtypeStruct(tile, F32), jax.Sh...]
where the time goes in v5:
time: 74.7 us; the launch traced here: 74.6 us
  Pallas kernels  73.4 us (98%)
  between operations  1.28 us (2%)
    pallas_call x1, Pallas kernels, on_device(): pl.pallas_call(kernel, out_shape=(jax.ShapeDtypeStruct(tile, F32), jax.Sh...  72.1 us

profile of v5, /device:TPU:1, one launch (start us, length us, event | category | flops | bytes accessed | tf_op | source)
XLA Modules:
  0.0 74.6 jit_solution(2354173692991246409)
XLA Ops:
  1.3 72.1 %coarray_subspace.1 = (f32[8,128]{1,0:T(8,128)S(1)}, f32[96,128]{1,0:T(8,128)S(1)}, f32[96,1024]{1,0:T(8,128)S(1)}) custom-call(s32[1]{0:T(128)S(6)} %copy.11.counts, s32[1,256]{1,0:T(1,128)} %bitcast.3, bf16[2,8,4096]{2,1,0:T(8,128)(2,1)} %bitcast.2, f32[2,96,512]{2,1,0:T(8,128)} %initial_in.1, bf16[2,512,256]{2,1,0:T(8,128)(2,1)} %constant.10.clone.forward_in, ...), custom_call_target="tpu_custom_call" | custom-call | tf_op jit(solution)/shard_map/coarray_subspace/pallas_call | solution.py:477
  73.4 1.2 %combine_columns.1 = (f32[2,512]{1,0:T(2,128)}, f32[2,96,512]{2,1,0:T(8,128)}) custom-call(f32[8,128]{1,0:T(8,128)S(1)} %get-tuple-element.5.lag_corr, f32[96,128]{1,0:T(8,128)S(1)} %get-tuple-element.6.inverse, f32[96,1024]{1,0:T(8,128)S(1)} %get-tuple-element.7.mapped), custom_call_target="tpu_custom_call" | custom-call | tf_op jit(solution)/shard_map/combine_columns/pallas_call | solution.py:525

commit v6 on v5

--- a/solution.py
+++ b/solution.py
@@ -170,7 +170,7 @@
     idle = jnp.logical_not(active)
     own_col = jnp.minimum(mine, OWN - 1)
     shifts = [(z, y) for z in range(LAG_Z) for y in range(LAG_Y) if z or y]
-    shifts.sort(key=lambda d: -(min(d[0], LAG_Z - d[0]) + min(d[1], LAG_Y - d[1])))
+    shifts.sort(key=lambda d: (-(min(d[0], LAG_Z - d[0]) + min(d[1], LAG_Y - d[1])), -min(d[1], LAG_Y - d[1])))
 
     loads = [
         pltpu.make_async_copy(src, dst, load_sems.at[i])
@@ -422,7 +422,11 @@
         to_lags(GRAM + 4 * sweep, lambda p: gram_send.at[sweep], gram_recv.at[sweep, me])
         drain(GRAM + 4 * sweep, gram_recv.at[sweep, pl.ds(0, N_LAG - 1)])
         gram_recv[sweep, me] = gram_send[sweep]
+    settled = list(drains)
+    drains.clear()
     rest = to_blocks(REST, ITERS - 1, range(REACH + 1, N_SNAP))
+    for finish in settled:
+        finish()
 
     for sweep in range(ITERS):
         wait(recv_sems, GRAM + 4 * sweep, gram_recv.at[sweep, pl.ds(0, N_LAG - 1)])

time: 74.7 us -> 74.1 us (level)
  no operation moved by 1% of the time
where the time goes in v6:
time: 74.1 us; the launch traced here: 74 us
  Pallas kernels  72.7 us (98%)
  between operations  1.28 us (2%)
    pallas_call x1, Pallas kernels, on_device(): pl.pallas_call(kernel, out_shape=(jax.ShapeDtypeStruct(tile, F32), jax.Sh...  71.5 us

profile of v6, /device:TPU:1, one launch (start us, length us, event | category | flops | bytes accessed | tf_op | source)
XLA Modules:
  0.0 74.0 jit_solution(13458133563419196217)
XLA Ops:
  1.3 71.5 %coarray_subspace.1 = (f32[8,128]{1,0:T(8,128)S(1)}, f32[96,128]{1,0:T(8,128)S(1)}, f32[96,1024]{1,0:T(8,128)S(1)}) custom-call(s32[1]{0:T(128)S(6)} %copy.11.counts, s32[1,256]{1,0:T(1,128)} %bitcast.3, bf16[2,8,4096]{2,1,0:T(8,128)(2,1)} %bitcast.2, f32[2,96,512]{2,1,0:T(8,128)} %initial_in.1, bf16[2,512,256]{2,1,0:T(8,128)(2,1)} %constant.10.clone.forward_in, ...), custom_call_target="tpu_custom_call" | custom-call | tf_op jit(solution)/shard_map/coarray_subspace/pallas_call | solution.py:481
  72.8 1.2 %combine_columns.1 = (f32[2,512]{1,0:T(2,128)}, f32[2,96,512]{2,1,0:T(8,128)}) custom-call(f32[8,128]{1,0:T(8,128)S(1)} %get-tuple-element.5.lag_corr, f32[96,128]{1,0:T(8,128)S(1)} %get-tuple-element.6.inverse, f32[96,1024]{1,0:T(8,128)S(1)} %get-tuple-element.7.mapped), custom_call_target="tpu_custom_call" | custom-call | tf_op jit(solution)/shard_map/combine_columns/pallas_call | solution.py:529

commit v7 on v6

--- a/solution.py
+++ b/solution.py
@@ -170,7 +170,7 @@
     idle = jnp.logical_not(active)
     own_col = jnp.minimum(mine, OWN - 1)
     shifts = [(z, y) for z in range(LAG_Z) for y in range(LAG_Y) if z or y]
-    shifts.sort(key=lambda d: (-(min(d[0], LAG_Z - d[0]) + min(d[1], LAG_Y - d[1])), -min(d[1], LAG_Y - d[1])))
+    shifts.sort(key=lambda d: (-min(d[0], LAG_Z - d[0]), -min(d[1], LAG_Y - d[1])))
 
     loads = [
         pltpu.make_async_copy(src, dst, load_sems.at[i])

time: 74.1 us -> 74.1 us (level)
  no operation moved by 1% of the time
where the time goes in v7:
time: 74.1 us; the launch traced here: 74 us
  Pallas kernels  72.7 us (98%)
  between operations  1.28 us (2%)
    pallas_call x1, Pallas kernels, on_device(): pl.pallas_call(kernel, out_shape=(jax.ShapeDtypeStruct(tile, F32), jax.Sh...  71.5 us

profile of v7, /device:TPU:1, one launch (start us, length us, event | category | flops | bytes accessed | tf_op | source)
XLA Modules:
  0.0 74.0 jit_solution(50942851070252674)
XLA Ops:
  1.3 71.5 %coarray_subspace.1 = (f32[8,128]{1,0:T(8,128)S(1)}, f32[96,128]{1,0:T(8,128)S(1)}, f32[96,1024]{1,0:T(8,128)S(1)}) custom-call(s32[1]{0:T(128)S(6)} %copy.11.counts, s32[1,256]{1,0:T(1,128)} %bitcast.3, bf16[2,8,4096]{2,1,0:T(8,128)(2,1)} %bitcast.2, f32[2,96,512]{2,1,0:T(8,128)} %initial_in.1, bf16[2,512,256]{2,1,0:T(8,128)(2,1)} %constant.10.clone.forward_in, ...), custom_call_target="tpu_custom_call" | custom-call | tf_op jit(solution)/shard_map/coarray_subspace/pallas_call | solution.py:481
  72.7 1.2 %combine_columns.1 = (f32[2,512]{1,0:T(2,128)}, f32[2,96,512]{2,1,0:T(8,128)}) custom-call(f32[8,128]{1,0:T(8,128)S(1)} %get-tuple-element.5.lag_corr, f32[96,128]{1,0:T(8,128)S(1)} %get-tuple-element.6.inverse, f32[96,1024]{1,0:T(8,128)S(1)} %get-tuple-element.7.mapped), custom_call_target="tpu_custom_call" | custom-call | tf_op jit(solution)/shard_map/combine_columns/pallas_call | solution.py:529
